TPU v7x, 32 devices: a whole 2x2x4 slice. The times are simulated.
32 devices in a mesh: head: 4 (over y, core), batch: 8 (over z, x).
Axes of the slice: x: 2, y: 2, z: 4, core: 2. Of those that a mesh axis runs over, the one named last changes fastest.
Arguments:
- tokens: bfloat16 [8, 2048, 1024], P('batch'), may hold values from -6 to 6
- seq_lengths: int32 [8, 4], P('batch'), may hold values from 0 to 2048, as said below
- qkv_weight: bfloat16 [3, 1024, 1024], P(None, None, 'head'), may hold values from -0.1875 to 0.1875
- out_weight: bfloat16 [1024, 1024], P('head'), may hold values from -0.1875 to 0.1875
- up_gate_weight: bfloat16 [2, 1024, 4096], P(None, None, 'head'), may hold values from -0.1875 to 0.1875
- down_weight: bfloat16 [4096, 1024], P('head'), may hold values from -0.09375 to 0.09375
- qk_scale: float32 [1024], P('head'), may hold values from 0.9 to 1.8
- mlp_scale: float32 [2, 4096], P(None, 'head'), may hold values from 0.5 to 2
- eigen_rates: float32 [1024, 2], replicated, may hold values from 0.05 to 0.6
- cotangent: bfloat16 [8, 2048, 1024], P('batch', 'head'), may hold values from -6 to 6
- block_order: int32 [4, 256], P('head'), may hold values from 0 to 255, each once within a row
- master_blocks: float32 [4, 256, 128, 128], P('head', 'batch'), may hold values from -0.1875 to 0.1875
- ema_blocks: float32 [4, 256, 128, 128], P('head', 'batch'), may hold values from -0.1875 to 0.1875
- left_stats: float32 [4, 256, 128, 128], P('head', 'batch'), as said below
- right_stats: float32 [4, 256, 128, 128], P('head', 'batch'), as said below
- left_root: float32 [4, 256, 128, 128], P('head', 'batch'), as said below
- right_root: float32 [4, 256, 128, 128], P('head', 'batch'), as said below
Outputs:
- block_out: float32 [8, 2048, 1024], P('batch', 'head')
- input_grad: float32 [8, 2048, 1024], P('batch', 'head')
- grad_blocks: float32 [4, 256, 128, 128], P('head', 'batch')
- new_master: float32 [4, 256, 128, 128], P('head', 'batch')
- new_ema: float32 [4, 256, 128, 128], P('head', 'batch')
- new_left: float32 [4, 256, 128, 128], P('head', 'batch')
- new_right: float32 [4, 256, 128, 128], P('head', 'batch')
- qk_scale_grad: float32 [1024], P('head')
- mlp_scale_out: float32 [2, 2, 4096], P(None, None, 'head')
- rate_grad: float32 [1024, 2], P('head')
- new_gains: float32 [3, 1024], P(None, 'head')
Inputs may be any that keep to these rules, and one draw needn't show every extreme that they name: `seq_lengths`: each row holds one sequence of 2048 tokens followed by zeros, or 4 sequences of 512 tokens; half of the rows are of each kind. `block_order`: each row names every block of its head group once. `left_stats`: each block is symmetric. `right_stats`: each block is symmetric. `left_root`: each block is symmetric. `right_root`: each block is symmetric.
All inputs are finite; a program needn't handle non-finite values.
Results may differ from a plain program's by a relative error of at most 0.02.
Values may be sent and summed in bfloat16 or wider, within the bound.
No kernel may reach another device: no remote copies, remote signals or barrier semaphores. Data moves between devices by JAX's collectives and lax.ppermute only.
A program may use at most 192 MiB of HBM per device.

v0:
```python
import math

import jax
import jax.numpy as jnp
from jax import lax
from jax.sharding import PartitionSpec as P

HEAD_DIM = 64
BLOCK = 128


def rms_rows(value):
    return value * lax.rsqrt(jnp.mean(value * value, axis=-1, keepdims=True) + 1e-06)


def rms_back(normed, value, gradient):
    factor = lax.rsqrt(jnp.mean(value * value, axis=-1, keepdims=True) + 1e-06)
    return factor * (gradient - normed * jnp.mean(gradient * normed, axis=-1, keepdims=True))


def positions_of(lengths_row, total_rows):
    ends = jnp.cumsum(lengths_row)
    starts = ends - lengths_row
    index = jnp.arange(total_rows, dtype=jnp.int32)
    segment = jnp.sum((index[:, None] >= ends[None, :]).astype(jnp.int32), axis=1)
    member = (
        segment[:, None] == jnp.arange(lengths_row.shape[0], dtype=jnp.int32)[None, :]
    ).astype(jnp.int32)
    begin = jnp.sum(member * starts[None, :], axis=1)
    return (segment, index - begin)


def rotate(value, positions, direction):
    half = HEAD_DIM // 2
    freq = 10000.0 ** (-jnp.arange(half, dtype=jnp.float32) * 2.0 / HEAD_DIM)
    angle = positions.astype(jnp.float32)[:, None] * freq[None, :]
    cosine = jnp.cos(angle)[:, None, :]
    sine = jnp.sin(angle)[:, None, :] * direction
    first = value[..., :half]
    second = value[..., half:]
    return jnp.concatenate(
        [first * cosine - second * sine, second * cosine + first * sine], axis=-1
    )


def shards(
    tokens,
    seq_lengths,
    qkv_weight,
    out_weight,
    up_gate_weight,
    down_weight,
    qk_scale,
    mlp_scale,
    eigen_rates,
    cotangent,
    block_order,
    master_blocks,
    ema_blocks,
    left_stats,
    right_stats,
    left_root,
    right_root,
):
    precise = lax.Precision.HIGHEST
    x_rows = tokens[0]
    tok_count = x_rows.shape[0]
    width = x_rows.shape[1]
    heads_here = qk_scale.shape[0] // HEAD_DIM
    head_size = lax.axis_size("head")
    share_rows = tok_count // head_size
    first_row = lax.axis_index("head") * share_rows
    segment, positions = positions_of(seq_lengths[0], tok_count)
    shape_heads = (tok_count, heads_here, HEAD_DIM)
    gains = qk_scale.reshape(heads_here, HEAD_DIM)
    projected = jnp.einsum("td,mdc->mtc", x_rows, qkv_weight, preferred_element_type=jnp.float32)
    q_rot = rotate(projected[0].reshape(shape_heads), positions, 1.0)
    k_rot = rotate(projected[1].reshape(shape_heads), positions, 1.0)
    q_hat = rms_rows(q_rot)
    k_hat = rms_rows(k_rot)
    q_used = (q_hat * gains).astype(jnp.bfloat16)
    k_used = (k_hat * gains).astype(jnp.bfloat16)
    v_used = projected[2].astype(jnp.bfloat16).reshape(shape_heads)
    block_rows = min(512, tok_count)
    score_scale = 1.0 / math.sqrt(HEAD_DIM)
    key_index = jnp.arange(tok_count, dtype=jnp.int32)
    offsets = jnp.arange(tok_count // block_rows, dtype=jnp.int32) * block_rows

    def block_scores(offset):
        q_block = lax.dynamic_slice_in_dim(q_used, offset, block_rows, 0)
        seg_block = lax.dynamic_slice_in_dim(segment, offset, block_rows, 0)
        row_index = offset + jnp.arange(block_rows, dtype=jnp.int32)
        scores = (
            jnp.einsum("qhd,khd->hqk", q_block, k_used, preferred_element_type=jnp.float32)
            * score_scale
        )
        allowed = (seg_block[:, None] == segment[None, :]) & (
            key_index[None, :] <= row_index[:, None]
        )
        return (jnp.where(allowed[None], scores, -1e30), q_block)

    def attend(offset):
        scores, q_block = block_scores(offset)
        row_max = jnp.max(scores, axis=-1, keepdims=True)
        weights = jnp.exp(scores - row_max)
        row_total = jnp.sum(weights, axis=-1, keepdims=True)
        probs = (weights / row_total).astype(jnp.bfloat16)
        result = jnp.einsum("hqk,khd->qhd", probs, v_used, preferred_element_type=jnp.float32)
        return (result.astype(jnp.bfloat16), (row_max + jnp.log(row_total))[..., 0])

    attn_blocks, log_total = lax.map(attend, offsets)
    attn_out = attn_blocks.reshape(tok_count, heads_here * HEAD_DIM)
    a_share = lax.psum_scatter(
        jnp.dot(attn_out, out_weight, preferred_element_type=jnp.float32).astype(jnp.bfloat16),
        "head",
        scatter_dimension=0,
        tiled=True,
    ).astype(jnp.float32)
    x_share = lax.dynamic_slice_in_dim(x_rows, first_row, share_rows, 0).astype(jnp.float32)
    h_attn = rms_rows(a_share)
    pre_attn = x_share + eigen_rates[:, 0] * (h_attn - x_share)
    hidden_share = rms_rows(pre_attn)
    hidden_low = hidden_share.astype(jnp.bfloat16)
    hidden_full = lax.all_gather(hidden_low, "head", axis=0, tiled=True)
    up_gate = jnp.einsum(
        "td,mdf->mtf", hidden_full, up_gate_weight, preferred_element_type=jnp.float32
    )
    up_proj = up_gate[0] * mlp_scale[0]
    gate_proj = up_gate[1] * mlp_scale[1]
    sigmoid_gate = jax.nn.sigmoid(gate_proj)
    activated = gate_proj * sigmoid_gate
    mixed = (up_proj * activated).astype(jnp.bfloat16)
    b_share = lax.psum_scatter(
        jnp.dot(mixed, down_weight, preferred_element_type=jnp.float32).astype(jnp.bfloat16),
        "head",
        scatter_dimension=0,
        tiled=True,
    ).astype(jnp.float32)
    h_mlp = rms_rows(b_share)
    pre_out = hidden_share + eigen_rates[:, 1] * (h_mlp - hidden_share)
    out_share = rms_rows(pre_out)
    grad_out_rows = cotangent[0].astype(jnp.float32)
    d_pre_out = rms_back(out_share, pre_out, grad_out_rows)
    d_h_mlp = eigen_rates[:, 1] * d_pre_out
    d_hidden = (1.0 - eigen_rates[:, 1]) * d_pre_out
    rate_mlp = jnp.sum(d_pre_out * (h_mlp - hidden_share), axis=0)
    d_branch_mlp = rms_back(h_mlp, b_share, d_h_mlp).astype(jnp.bfloat16)
    d_mlp_rows = lax.all_gather(d_branch_mlp, "head", axis=0, tiled=True)
    d_mixed = jnp.einsum("tD,fD->tf", d_mlp_rows, down_weight, preferred_element_type=jnp.float32)
    grad_down = jnp.einsum("tf,tD->fD", mixed, d_mlp_rows, preferred_element_type=jnp.float32)
    d_up = d_mixed * activated
    d_gate = d_mixed * up_proj * sigmoid_gate * (1.0 + gate_proj * (1.0 - sigmoid_gate))
    grad_scales = jnp.stack(
        [jnp.sum(d_up * up_gate[0], axis=0), jnp.sum(d_gate * up_gate[1], axis=0)]
    )
    d_up_gate = jnp.stack([d_up * mlp_scale[0], d_gate * mlp_scale[1]]).astype(jnp.bfloat16)
    grad_up_gate = jnp.einsum(
        "td,mtf->mdf", hidden_full, d_up_gate, preferred_element_type=jnp.float32
    )
    d_hidden = d_hidden + lax.psum_scatter(
        jnp.einsum(
            "mtf,mdf->td", d_up_gate, up_gate_weight, preferred_element_type=jnp.float32
        ).astype(jnp.bfloat16),
        "head",
        scatter_dimension=0,
        tiled=True,
    ).astype(jnp.float32)
    d_pre_attn = rms_back(hidden_share, pre_attn, d_hidden)
    d_h_attn = eigen_rates[:, 0] * d_pre_attn
    d_input = (1.0 - eigen_rates[:, 0]) * d_pre_attn
    rate_attn = jnp.sum(d_pre_attn * (h_attn - x_share), axis=0)
    d_branch_attn = rms_back(h_attn, a_share, d_h_attn).astype(jnp.bfloat16)
    d_attn_rows = lax.all_gather(d_branch_attn, "head", axis=0, tiled=True)
    grad_out = jnp.einsum("tc,tD->cD", attn_out, d_attn_rows, preferred_element_type=jnp.float32)
    d_attn = (
        jnp.einsum("tD,cD->tc", d_attn_rows, out_weight, preferred_element_type=jnp.float32)
        .astype(jnp.bfloat16)
        .reshape(shape_heads)
    )

    def attend_back(carry, item):
        dk_total, dv_total = carry
        offset, log_block = item
        scores, q_block = block_scores(offset)
        probs = jnp.exp(scores - log_block[..., None])
        d_out_block = lax.dynamic_slice_in_dim(d_attn, offset, block_rows, 0)
        dv_total = dv_total + jnp.einsum(
            "hqk,qhd->khd",
            probs.astype(jnp.bfloat16),
            d_out_block,
            preferred_element_type=jnp.float32,
        )
        d_probs = jnp.einsum(
            "qhd,khd->hqk", d_out_block, v_used, preferred_element_type=jnp.float32
        )
        delta = jnp.sum(probs * d_probs, axis=-1, keepdims=True)
        d_scores = (probs * (d_probs - delta)).astype(jnp.bfloat16)
        dq_block = (
            jnp.einsum("hqk,khd->qhd", d_scores, k_used, preferred_element_type=jnp.float32)
            * score_scale
        )
        dk_total = (
            dk_total
            + jnp.einsum("hqk,qhd->khd", d_scores, q_block, preferred_element_type=jnp.float32)
            * score_scale
        )
        return ((dk_total, dv_total), dq_block)

    zero_heads = jnp.zeros(shape_heads, jnp.float32)
    (dk_used, dv_raw), dq_blocks = lax.scan(
        attend_back, (zero_heads, zero_heads), (offsets, log_total)
    )
    dq_used = dq_blocks.reshape(shape_heads)
    grad_gain = (jnp.sum(dq_used * q_hat, axis=0) + jnp.sum(dk_used * k_hat, axis=0)).reshape(-1)
    dq_raw = rotate(rms_back(q_hat, q_rot, dq_used * gains), positions, -1.0)
    dk_raw = rotate(rms_back(k_hat, k_rot, dk_used * gains), positions, -1.0)
    flat_shape = (tok_count, heads_here * HEAD_DIM)
    d_projected = jnp.stack(
        [dq_raw.reshape(flat_shape), dk_raw.reshape(flat_shape), dv_raw.reshape(flat_shape)]
    ).astype(jnp.bfloat16)
    grad_qkv = jnp.einsum("td,mtc->mdc", x_rows, d_projected, preferred_element_type=jnp.float32)
    d_input_part = jnp.einsum(
        "mtc,mdc->td", d_projected, qkv_weight, preferred_element_type=jnp.float32
    )
    rate_grad = jnp.stack([rate_attn, rate_mlp], axis=1)
    d_input_share, rate_share = (
        lax.psum_scatter(
            d_input_part.astype(jnp.bfloat16), "head", scatter_dimension=0, tiled=True
        ).astype(jnp.float32),
        lax.psum_scatter(
            rate_grad.astype(jnp.bfloat16), "head", scatter_dimension=0, tiled=True
        ).astype(jnp.float32),
    )
    d_input = d_input + d_input_share
    matrix = jnp.concatenate(
        [
            grad_qkv[0],
            grad_qkv[1],
            grad_qkv[2],
            grad_out.T,
            grad_up_gate[0],
            grad_up_gate[1],
            grad_down.T,
        ],
        axis=1,
    )
    row_blocks = width // BLOCK
    panels = matrix.shape[1] // BLOCK
    blocks = (
        matrix.reshape(row_blocks, BLOCK, panels, BLOCK)
        .transpose(2, 0, 1, 3)
        .reshape(-1, BLOCK, BLOCK)
    )
    slot_order = block_order[0]
    ordered = jnp.take(blocks, slot_order, axis=0)
    owners = lax.axis_size("batch")
    per_owner = ordered.shape[0] // owners
    pieces = lax.psum_scatter(
        ordered.astype(jnp.bfloat16), "batch", scatter_dimension=1, tiled=True
    ).astype(jnp.float32)
    owned_grad = lax.all_to_all(
        pieces.astype(jnp.bfloat16), "batch", split_axis=0, concat_axis=1, tiled=True
    ).astype(pieces.dtype)
    new_left = 0.5 * left_stats[0] + 0.5 * jnp.einsum(
        "sij,skj->sik", owned_grad, owned_grad, precision=precise
    )
    new_right = 0.5 * right_stats[0] + 0.5 * jnp.einsum(
        "sji,sjk->sik", owned_grad, owned_grad, precision=precise
    )
    direction = jnp.einsum("sij,sjk->sik", left_root[0], owned_grad, precision=precise)
    direction = jnp.einsum("sij,sjk->sik", direction, right_root[0], precision=precise)
    stepped = master_blocks[0] - 0.3 * direction
    column_sq = jnp.sum(stepped * stepped, axis=1)
    my_blocks = lax.dynamic_slice_in_dim(
        slot_order, lax.axis_index("batch") * per_owner, per_owner, 0
    )
    member = (
        (my_blocks // row_blocks)[:, None] == jnp.arange(panels, dtype=jnp.int32)[None, :]
    ).astype(jnp.float32)
    panel_sq = jnp.einsum("sp,sb->pb", member, column_sq, precision=precise)
    totals, gain_sum, scale_sum, rate_sum = lax.psum(
        (panel_sq, grad_gain, grad_scales, rate_share), "batch"
    )
    norms = jnp.einsum("sp,pb->sb", member, totals, precision=precise)
    new_master = stepped * lax.rsqrt(norms + 1e-06)[:, None, :]
    new_ema = 0.5 * ema_blocks[0] + 0.5 * new_master
    gain_step = 0.5 / math.sqrt(tok_count * owners)
    width_share = width // head_size
    rate_slice = lax.dynamic_slice_in_dim(
        eigen_rates, lax.axis_index("head") * width_share, width_share, 0
    )
    mlp_scale_out = jnp.stack([scale_sum, mlp_scale - gain_step * scale_sum])
    new_gains = jnp.concatenate(
        [(qk_scale - gain_step * gain_sum)[None, :], (rate_slice - gain_step * rate_sum).T], axis=0
    )
    return (
        out_share[None],
        d_input[None],
        owned_grad[None],
        new_master[None],
        new_ema[None],
        new_left[None],
        new_right[None],
        gain_sum,
        mlp_scale_out,
        rate_sum,
        new_gains,
    )


def solution(mesh):
    return jax.shard_map(
        shards,
        mesh=mesh,
        in_specs=(
            P("batch", None, None),
            P("batch", None),
            P(None, None, "head"),
            P("head", None),
            P(None, None, "head"),
            P("head", None),
            P("head"),
            P(None, "head"),
            P(),
            P("batch", "head", None),
            P("head", None),
            P("head", "batch", None, None),
            P("head", "batch", None, None),
            P("head", "batch", None, None),
            P("head", "batch", None, None),
            P("head", "batch", None, None),
            P("head", "batch", None, None),
        ),
        out_specs=(
            P("batch", "head", None),
            P("batch", "head", None),
            P("head", "batch", None, None),
            P("head", "batch", None, None),
            P("head", "batch", None, None),
            P("head", "batch", None, None),
            P("head", "batch", None, None),
            P("head"),
            P(None, None, "head"),
            P("head", None),
            P(None, "head"),
        ),
        check_vma=False,
    )
```

profile of v0, /device:TPU:0, one launch (start us, length us, event | category | flops | bytes accessed | tf_op | source)
XLA Modules:
  0.0 1112.9 jit_solution(16494868616636362357)
XLA Ops:
  28.2 77.9 %while.28 = (s32[]{:T(128)}, bf16[4,512,4,64]{1,3,2,0:T(8,128)(2,1)}, f32[4,4,512]{2,1,0:T(4,128)S(1)}, s32[4]{0:T(128)S(1)}, s32[2048]{0:T(1024)S(1)}, /*index=...) while((s32[]{:T(128)}, ...), condition=%wide.region_8.9_spmd.clone, body=%wide.region_5.8_spmd.clone.sunk | while | flops 1127348736 | bytes 61426372 | solution.py:111
  113.4 46.8 %reduce-scatter.9.cloned.1.call-done = bf16[512,1024]{1,0:T(8,128)(2,1)} async-done(((bf16[2048,1024]{1,0:T(8,128)(2,1)}), bf16[512,1024]{1,0:T(8,128)(2,1)}) %reduce-scatter.9.cloned.1.call-update) | async-done | bytes 1048592 | tf_op jit(solution)/shard_map/reduce_scatter | solution.py:113
  167.1 34.5 %all-gather.4.cloned.1.call-done = bf16[2048,1024]{1,0:T(8,128)(2,1)} async-done(((bf16[512,1024]{1,0:T(8,128)(2,1)}), bf16[2048,1024]{1,0:T(8,128)(2,1)}) %all-gather.4.cloned.1.call-update) | async-done | bytes 4194320 | tf_op jit(solution)/shard_map/all_gather | solution.py:124
  201.7 14.8 %convolution_bitcast_fusion = f32[2,2048,1024]{2,1,0:T(8,128)S(1)} fusion(bf16[2,1024,1024]{2,1,0:T(8,128)(2,1)} %param.25, bf16[2048,1024]{1,0:T(8,128)(2,1)} %all-gather.4.cloned.1.call-done), kind=kOutput, calls=%fused_computation.66 | convolution fusion | flops 8589934592 | bytes 25165824 | tf_op jit(solution)/shard_map/td,mdf->mtf/dot_general | solution.py:125
  230.8 44.7 %reduce-scatter.11.cloned.1.call-done = bf16[512,1024]{1,0:T(8,128)(2,1)} async-done(((bf16[2048,1024]{1,0:T(8,128)(2,1)}), bf16[512,1024]{1,0:T(8,128)(2,1)}) %reduce-scatter.11.cloned.1.call-update) | async-done | bytes 1048592 | tf_op jit(solution)/shard_map/reduce_scatter | solution.py:133
  288.4 34.6 %all-gather.6.cloned.1.call-done = bf16[2048,1024]{1,0:T(8,128)(2,1)} async-done(((bf16[512,1024]{1,0:T(8,128)(2,1)}), bf16[2048,1024]{1,0:T(8,128)(2,1)}) %all-gather.6.cloned.1.call-update) | async-done | bytes 4194320 | tf_op jit(solution)/shard_map/all_gather | solution.py:148
  323.0 20.1 %multiply_reduce_fusion.2 = (f32[1024]{0:T(1024)}, f32[1024]{0:T(1024)}, f32[2048,1024]{1,0:T(8,128)S(1)}, bf16[1,2048,1024]{2,1,0:T(8,128)(2,1)}) fusion(f32[2,2048,1024]{2,1,0:T(8,128)} %copy-done.26, f32[1024]{0:T(1024)S(1)} %bitcast.351, f32[1024]{0:T(1024)S(1)} %bitcast.355, bf16[2048,1024]{1,0:T(8,128)(2,1)} %all-gather.6.cloned.1.call-done, ...), kind=kOutput, calls=%fused_computation.57 | convolution fusion | flops 4334811136 | bytes 35667968 | tf_op jit(solution)/shard_map/tD,fD->tf/dot_general | solution.py:149
  358.5 44.7 %reduce-scatter.13.cloned.1.call-done = bf16[512,1024]{1,0:T(8,128)(2,1)} async-done(((bf16[2048,1024]{1,0:T(8,128)(2,1)}), bf16[512,1024]{1,0:T(8,128)(2,1)}) %reduce-scatter.13.cloned.1.call-update) | async-done | bytes 1048592 | tf_op jit(solution)/shard_map/reduce_scatter | solution.py:160
  421.6 14.9 %fusion.60 = bf16[2,1024,1024]{1,2,0:T(8,128)(2,1)} fusion(bf16[2048,1024]{1,0:T(8,128)(2,1)} %all-gather.4.cloned.1.call-done, bf16[1,2048,1024]{2,1,0:T(8,128)(2,1)} %copy-done.35, bf16[1,2048,1024]{2,1,0:T(8,128)(2,1)} %get-tuple-element.242), kind=kOutput, calls=%fused_computation.84 | convolution fusion | flops 8594128896 | bytes 16777216 | tf_op jit(solution)/shard_map/td,mtf->mdf/dot_general | solution.py:157
  436.5 14.5 %all-gather.8.cloned.1.call-done = bf16[2048,1024]{1,0:T(8,128)(2,1)} async-done(((bf16[512,1024]{1,0:T(8,128)(2,1)}), bf16[2048,1024]{1,0:T(8,128)(2,1)}) %all-gather.8.cloned.1.call-update) | async-done | bytes 4194320 | tf_op jit(solution)/shard_map/all_gather | solution.py:173
  455.6 289.8 %while.29 = (s32[]{:T(128)}, f32[2048,4,64]{0,2,1:T(8,128)}, f32[2048,4,64]{0,2,1:T(8,128)}, f32[4,512,4,64]{1,0,3,2:T(4,128)}, s32[4]{0:T(128)S(1)}, /*index=5*...) while((s32[]{:T(128)}, f32[2048,4,64]{0,2,1:T(8,128)}, ...), condition=%wide.region_22.23_spmd.clone, body=%wide.region_20.22_spmd.clone.sunk | while | flops 2753165824 | bytes 183052560 | solution.py:210
  469.3 12.6 %multiply_reduce_fusion.16 = (f32[4,512]{1,0:T(4,128)S(1)}, f32[4,512,2048]{2,1,0:T(8,128)}) fusion(f32[4,512,2048]{2,1,0:T(8,128)} %fusion.180, f32[4,512]{1,0:T(4,128)S(1)} %dynamic-slice_bitcast_fusion.2, pred[512,2048]{1,0:T(8,128)(4,1)S(1)} %fusion.181, bf16[2048,4,64]{0,2,1:T(8,128)(2,1)S(1)} %get-tuple-element.469, ...), kind=kOutput, calls=%fused_computation.22.clone.1 | convolution fusion | flops 557840384 | bytes 35930116 | tf_op jit(solution)/shard_map/while/body/eval_jaxpr/qhd,khd->hqk/dot_general | solution.py:193
  540.7 12.6 %multiply_reduce_fusion.16 = (f32[4,512]{1,0:T(4,128)S(1)}, f32[4,512,2048]{2,1,0:T(8,128)}) fusion(f32[4,512,2048]{2,1,0:T(8,128)} %fusion.180, f32[4,512]{1,0:T(4,128)S(1)} %dynamic-slice_bitcast_fusion.2, pred[512,2048]{1,0:T(8,128)(4,1)S(1)} %fusion.181, bf16[2048,4,64]{0,2,1:T(8,128)(2,1)S(1)} %get-tuple-element.469, ...), kind=kOutput, calls=%fused_computation.22.clone.1 | convolution fusion | flops 557840384 | bytes 35930116 | tf_op jit(solution)/shard_map/while/body/eval_jaxpr/qhd,khd->hqk/dot_general | solution.py:193
  587.3 12.5 %fusion.183 = f32[2048,4,64]{0,2,1:T(8,128)} fusion(f32[4,512,2048]{2,1,0:T(8,128)} %fusion.180, f32[4,512]{1,0:T(4,128)S(1)} %dynamic-slice_bitcast_fusion.2, pred[512,2048]{1,0:T(8,128)(4,1)S(1)} %fusion.181, f32[2048,4,64]{0,2,1:T(8,128)} %get-tuple-element.447, pred[]{:T(512)S(6)} %compare.10, bf16[2048,4,64]{0,2,1:T(8,128)(2,1)} %get-tuple-element.468, ...), kind=kOutput, calls=%fused_computation.33.clone.1 | convolution fusion | flops 554696704 | bytes 22290436 | tf_op jit(solution)/shard_map/while/body/eval_jaxpr/hqk,qhd->khd/dot_general | solution.py:187
  613.3 12.6 %multiply_reduce_fusion.16 = (f32[4,512]{1,0:T(4,128)S(1)}, f32[4,512,2048]{2,1,0:T(8,128)}) fusion(f32[4,512,2048]{2,1,0:T(8,128)} %fusion.180, f32[4,512]{1,0:T(4,128)S(1)} %dynamic-slice_bitcast_fusion.2, pred[512,2048]{1,0:T(8,128)(4,1)S(1)} %fusion.181, bf16[2048,4,64]{0,2,1:T(8,128)(2,1)S(1)} %get-tuple-element.469, ...), kind=kOutput, calls=%fused_computation.22.clone.1 | convolution fusion | flops 557840384 | bytes 35930116 | tf_op jit(solution)/shard_map/while/body/eval_jaxpr/qhd,khd->hqk/dot_general | solution.py:193
  660.0 12.5 %fusion.183 = f32[2048,4,64]{0,2,1:T(8,128)} fusion(f32[4,512,2048]{2,1,0:T(8,128)} %fusion.180, f32[4,512]{1,0:T(4,128)S(1)} %dynamic-slice_bitcast_fusion.2, pred[512,2048]{1,0:T(8,128)(4,1)S(1)} %fusion.181, f32[2048,4,64]{0,2,1:T(8,128)} %get-tuple-element.447, pred[]{:T(512)S(6)} %compare.10, bf16[2048,4,64]{0,2,1:T(8,128)(2,1)} %get-tuple-element.468, ...), kind=kOutput, calls=%fused_computation.33.clone.1 | convolution fusion | flops 554696704 | bytes 22290436 | tf_op jit(solution)/shard_map/while/body/eval_jaxpr/hqk,qhd->khd/dot_general | solution.py:187
  685.9 12.6 %multiply_reduce_fusion.16 = (f32[4,512]{1,0:T(4,128)S(1)}, f32[4,512,2048]{2,1,0:T(8,128)}) fusion(f32[4,512,2048]{2,1,0:T(8,128)} %fusion.180, f32[4,512]{1,0:T(4,128)S(1)} %dynamic-slice_bitcast_fusion.2, pred[512,2048]{1,0:T(8,128)(4,1)S(1)} %fusion.181, bf16[2048,4,64]{0,2,1:T(8,128)(2,1)S(1)} %get-tuple-element.469, ...), kind=kOutput, calls=%fused_computation.22.clone.1 | convolution fusion | flops 557840384 | bytes 35930116 | tf_op jit(solution)/shard_map/while/body/eval_jaxpr/qhd,khd->hqk/dot_general | solution.py:193
  732.5 12.4 %fusion.183 = f32[2048,4,64]{0,2,1:T(8,128)} fusion(f32[4,512,2048]{2,1,0:T(8,128)} %fusion.180, f32[4,512]{1,0:T(4,128)S(1)} %dynamic-slice_bitcast_fusion.2, pred[512,2048]{1,0:T(8,128)(4,1)S(1)} %fusion.181, f32[2048,4,64]{0,2,1:T(8,128)} %get-tuple-element.447, pred[]{:T(512)S(6)} %compare.10, bf16[2048,4,64]{0,2,1:T(8,128)(2,1)} %get-tuple-element.468, ...), kind=kOutput, calls=%fused_computation.33.clone.1 | convolution fusion | flops 554696704 | bytes 22290436 | tf_op jit(solution)/shard_map/while/body/eval_jaxpr/hqk,qhd->khd/dot_general | solution.py:187
  796.1 12.5 %copy.106 = bf16[8,128,32,128]{3,1,0,2:T(8,128)(2,1)} copy(bf16[8,128,32,128]{1,0,3,2:T(8,128)(2,1)} %bitcast.319) | data formatting | bytes 16777216 | tf_op jit(solution)/shard_map/reshape | solution.py:250
  808.6 12.1 %gather_fusion = bf16[256,128,128]{2,1,0:T(8,128)(2,1)} fusion(bf16[256,128,128]{2,1,0:T(8,128)(2,1)} %bitcast.318, s32[1024]{0:T(1024)} %pad_clamp_fusion), kind=kCustom, calls=%fused_computation | custom fusion | bytes 16778240 | tf_op jit(solution)/shard_map/jit(_take)/gather | solution.py:255
  837.5 139.6 %reduce-scatter.17.cloned.1.call-done = bf16[256,16,128]{2,1,0:T(8,128)(2,1)} async-done(((bf16[256,128,128]{2,1,0:T(8,128)(2,1)}), bf16[256,16,128]{2,1,0:T(8,128)(2,1)}) %reduce-scatter.17.cloned.1.call-update) | async-done | bytes 1048592 | tf_op jit(solution)/shard_map/reduce_scatter | solution.py:258
  981.2 18.1 %reduce-scatter.19.cloned.1.call-done = bf16[256,2]{1,0:T(8,128)(2,1)} async-done(((bf16[1024,2]{1,0:T(8,128)(2,1)}), bf16[256,2]{1,0:T(8,128)(2,1)}) %reduce-scatter.19.cloned.1.call-update) | async-done | bytes 1040
  1000.3 46.1 %reduce-scatter.15.cloned.1.call-done = bf16[512,1024]{1,0:T(8,128)(2,1)} async-done(((bf16[2048,1024]{1,0:T(8,128)(2,1)}), bf16[512,1024]{1,0:T(8,128)(2,1)}) %reduce-scatter.15.cloned.1.call-update) | async-done | bytes 1048592 | tf_op jit(solution)/shard_map/reduce_scatter | solution.py:227
  1058.6 37.1 %all-reduce = (f32[32,128]{1,0:T(8,128)S(1)}, f32[256]{0:T(256)S(1)}, f32[2,1024]{1,0:T(2,128)S(1)}, f32[256,2]{0,1:T(2,128)S(1)}) all-reduce(f32[32,128]{1,0:T(8,128)S(1)} %fusion.101, f32[256]{0:T(256)S(1)} %add.250, f32[2,1024]{1,0:T(2,128)S(1)} %pad_maximum_fusion.15, ...), channel_id=1, replica_groups=mesh['head'=4,'batch'=8] {'batch'}, use_global_device_ids=true, to_apply=%region_28.29 | all-reduce | flops 6912 | bytes 54272 | tf_op jit(solution)/shard_map/psum | solution.py:281
  (377 shorter events, 458.9 us)
Async XLA Ops:
  7.2 217.4 %copy-start = (bf16[1024,1024]{1,0:T(8,128)(2,1)S(1)}, bf16[1024,1024]{1,0:T(8,128)(2,1)}, u32[]{:S(2)}) copy-start(bf16[1024,1024]{1,0:T(8,128)(2,1)} %param.26) | copy-start | bytes 6291460
  7.2 152.9 %reduce-scatter.9.cloned.1.call-start = ((), (), s32[]{:S(2)}) async-start(), calls=%async_computation.7 | async-start | bytes 5242880 | tf_op jit(solution)/shard_map/reduce_scatter | solution.py:113
  112.7 89.0 %all-gather.4.cloned.1.call-start = ((), (), s32[]{:S(2)}) async-start(), calls=%async_computation.8 | async-start | bytes 5242880 | tf_op jit(solution)/shard_map/all_gather | solution.py:124
  113.4 300.1 %copy-start.54 = (f32[1024,1]{0,1:T(1,128)}, f32[1024,1]{0,1:T(1,128)S(1)}, u32[]{:S(2)}) copy-start(f32[1024,1]{0,1:T(1,128)S(1)} %get-tuple-element.264) | copy-start | bytes 12292
  167.0 108.4 %reduce-scatter.11.cloned.1.call-start = ((), (), s32[]{:S(2)}) async-start(), calls=%async_computation.9 | async-start | bytes 5242880 | tf_op jit(solution)/shard_map/reduce_scatter | solution.py:133
  230.7 92.2 %all-gather.6.cloned.1.call-start = ((), (), s32[]{:S(2)}) async-start(), calls=%async_computation.10 | async-start | bytes 5242880 | tf_op jit(solution)/shard_map/all_gather | solution.py:148
  288.4 114.9 %reduce-scatter.13.cloned.1.call-start = ((), (), s32[]{:S(2)}) async-start(), calls=%async_computation.11 | async-start | bytes 5242880 | tf_op jit(solution)/shard_map/reduce_scatter | solution.py:160
  358.5 44.8 %copy-start.5 = (bf16[512,1024]{1,0:T(8,128)(2,1)S(1)}, bf16[512,1024]{1,0:T(8,128)(2,1)}, u32[]{:S(2)}) copy-start(bf16[512,1024]{1,0:T(8,128)(2,1)} %reduce-scatter.9.cloned.1.call-done) | copy-start | bytes 3145732
  358.5 44.8 %copy-start.8 = (bf16[512,1024]{1,0:T(8,128)(2,1)S(1)}, bf16[512,1024]{1,0:T(8,128)(2,1)}, u32[]{:S(2)}) copy-start(bf16[512,1024]{1,0:T(8,128)(2,1)} %reduce-scatter.11.cloned.1.call-done) | copy-start | bytes 3145732
  358.5 92.5 %all-gather.8.cloned.1.call-start = ((), (), s32[]{:S(2)}) async-start(), calls=%async_computation.12 | async-start | bytes 5242880 | tf_op jit(solution)/shard_map/all_gather | solution.py:173
  416.4 560.7 %reduce-scatter.17.cloned.1.call-start = ((), (), s32[]{:S(2)}) async-start(), calls=%async_computation.14 | async-start | bytes 9437184 | tf_op jit(solution)/shard_map/reduce_scatter | solution.py:258
  421.6 29.4 %copy-start.53 = (bf16[256,1024]{1,0:T(8,128)(2,1)S(1)}, bf16[256,1024]{1,0:T(8,128)(2,1)}, u32[]{:S(2)}) copy-start(bf16[256,1024]{1,0:T(8,128)(2,1)} %param.24) | copy-start | bytes 1572868
  436.5 19.0 %copy-start.10 = (bf16[2048,4,64]{0,2,1:T(8,128)(2,1)S(1)}, bf16[2048,4,64]{0,2,1:T(8,128)(2,1)}, u32[]{:S(2)}) copy-start(bf16[2048,4,64]{0,2,1:T(8,128)(2,1)} %get-tuple-element.485) | copy-start | bytes 3145732
  587.3 12.5 %copy-start.11 = (bf16[2048,4,64]{0,2,1:T(8,128)(2,1)S(1)}, bf16[2048,4,64]{0,2,1:T(8,128)(2,1)}, u32[]{:S(2)}) copy-start(bf16[2048,4,64]{0,2,1:T(8,128)(2,1)} %get-tuple-element.500) | copy-start | bytes 3145732 | tf_op jit(solution)/shard_map/while
  829.1 170.2 %reduce-scatter.19.cloned.1.call-start = ((), (), s32[]{:S(2)}) async-start(), calls=%async_computation.15 | async-start | bytes 327680
  830.7 215.8 %reduce-scatter.15.cloned.1.call-start = ((), (), s32[]{:S(2)}) async-start(), calls=%async_computation.13 | async-start | bytes 5242880 | tf_op jit(solution)/shard_map/reduce_scatter | solution.py:227
  837.4 143.6 %copy-start.71 = (s32[1,256]{1,0:T(1,128)S(1)}, s32[1,256]{1,0:T(1,128)}, u32[]{:S(2)}) copy-start(s32[1,256]{1,0:T(1,128)} %param.31) | copy-start | bytes 3076
  837.4 143.7 %copy-start.55 = (f32[1024,1]{0,1:T(1,128)S(1)}, f32[1024,1]{0,1:T(1,128)}, u32[]{:S(2)}) copy-start(f32[1024,1]{0,1:T(1,128)} %copy-done.54) | copy-start | bytes 12292
  837.5 143.7 %copy-start.66 = (f32[1024]{0:T(1024)S(1)}, f32[1024]{0:T(1024)}, u32[]{:S(2)}) copy-start(f32[1024]{0:T(1024)} %get-tuple-element.184) | copy-start | bytes 12292
  837.5 143.7 %copy-start.67 = (f32[1024]{0:T(1024)S(1)}, f32[1024]{0:T(1024)}, u32[]{:S(2)}) copy-start(f32[1024]{0:T(1024)} %get-tuple-element.185) | copy-start | bytes 12292
  837.5 209.0 %copy-start.25 = (f32[512,1024]{1,0:T(8,128)S(1)}, f32[512,1024]{1,0:T(8,128)}, u32[]{:S(2)}) copy-start(f32[512,1024]{1,0:T(8,128)} %copy-done.24) | copy-start | bytes 6291460
  977.1 72.4 %all-to-all-start = ((bf16[256,16,128]{2,1,0:T(8,128)(2,1)}), bf16[256,16,128]{2,1,0:T(8,128)(2,1)S(1)}, u32[]{:S(2)}, u32[]{:S(2)}) async-start(bf16[256,16,128]{2,1,0:T(8,128)(2,1)} %reduce-scatter.17.cloned.1.call-done), calls=%async_computation.5 | async-start | bytes 2097152 | tf_op jit(solution)/shard_map/all_to_all | solution.py:261
  1054.4 41.3 %copy-start.65 = (f32[256]{0:T(256)S(1)}, f32[256]{0:T(256)}, u32[]{:S(2)}) copy-start(f32[256]{0:T(256)} %param.27) | copy-start | bytes 3076
  1054.4 41.3 %copy-start.60 = (f32[2,1024]{1,0:T(2,128)S(1)}, f32[2,1024]{1,0:T(2,128)}, u32[]{:S(2)}) copy-start(f32[2,1024]{1,0:T(2,128)} %param.28) | copy-start | bytes 24580
  (72 other events, 264.6 us)
Sparse Core Ops, SparseCore 0:
  112.8 47.2 reduce-scatter.8
  167.2 34.4 all-gather.3
  230.9 44.5 reduce-scatter.10
  288.5 34.4 all-gather.5
  358.6 44.5 reduce-scatter.12
  416.5 34.4 all-gather.7
  829.2 147.8 reduce-scatter.16
  980.1 19.1 reduce-scatter.18
  1001.9 44.5 reduce-scatter.14
where the time goes:
time: 1120 us; the launch traced here: 1110 us
  waiting for transfers between devices  424 us (38%)
  matrix products  331 us (30%)
  other arithmetic  153 us (14%)
  local copies, waits for them, and re-layouts  132 us (12%)
  blocking collectives  37.1 us (3%)
  loops' own time  16.2 us (1%)
  between operations  14.9 us (1%)
    reduce_scatter x1, waiting for transfers between devices, shards(): lax.psum_scatter(ordered.astype(jnp.bfloat16), 'batch', scatter_dimension...  140 us
    dot_general x8, matrix products, block_scores(): jnp.einsum('qhd,khd->hqk', q_block, k_used, preferred_element_type=jnp.fl...  55.2 us
    dot_general x4, matrix products, attend_back(): jnp.einsum('qhd,khd->hqk', d_out_block, v_used, preferred_element_type=jn...  50.3 us
    dot_general x4, matrix products, attend_back(): jnp.einsum('hqk,qhd->khd', probs.astype(jnp.bfloat16), d_out_block, prefe...  49.2 us
    convert_element_type x4, other arithmetic, attend_back(): d_scores = (probs * (d_probs - delta)).astype(jnp.bfloat16)  48.3 us
    reduce_scatter x1, waiting for transfers between devices, shards(): lax.psum_scatter(jnp.dot(attn_out, out_weight, preferred_element_type=jnp...  46.8 us
    dynamic_update_slice x8, local copies, waits for them, and re-layouts, shards(): lax.scan(attend_back, (zero_heads, zero_heads), (offsets, log_total))  46.5 us
    reduce_scatter x1, waiting for transfers between devices, shards(): lax.psum_scatter(d_input_part.astype(jnp.bfloat16), 'head', scatter_dimen...  46.1 us
  transfers between devices with their start and end apart: 10, of which 9 were waited for; matrix products, arithmetic and copies ran while one was open for 3% of the time, Pallas kernels for 0%

commit v1 on v0

v1 whole, which is shorter than its diff:
```python
import functools
import math

import jax
import jax.numpy as jnp
from jax import lax
from jax.experimental import pallas as pl
from jax.experimental.pallas import tpu as pltpu
from jax.sharding import PartitionSpec as P

HEAD_DIM = 64
BLOCK = 128
LANES = 128
CHUNKS = 2
F32 = jnp.float32
BF16 = jnp.bfloat16
NN = (((1,), (0,)), ((), ()))
NT = (((1,), (1,)), ((), ()))
TN = (((0,), (0,)), ((), ()))


def mm(a, b, dims=NN):
    return lax.dot_general(a, b, dims, preferred_element_type=F32)


def whole(shape, single=False):
    zeros = (0,) * len(shape)
    if single:
        return pl.BlockSpec(shape, lambda *_: zeros, pipeline_mode=pl.Buffered(1))
    return pl.BlockSpec(shape, lambda *_: zeros)


def rms_rows(value):
    return value * lax.rsqrt(jnp.mean(value * value, axis=-1, keepdims=True) + 1e-06)


def rms_factor(value):
    return lax.rsqrt(jnp.mean(value * value, axis=-1, keepdims=True) + 1e-06)


def rms_back(normed, factor, gradient):
    return factor * (gradient - normed * jnp.mean(gradient * normed, axis=-1, keepdims=True))


def lane_ids():
    return lax.broadcasted_iota(jnp.int32, (1, LANES), 1)


def head_mean(value, ones_block):
    high = value.astype(BF16)
    rest = (value - high.astype(F32)).astype(BF16)
    return (mm(high, ones_block) + mm(rest, ones_block)) * (1.0 / HEAD_DIM)


def ones_block():
    row = lax.broadcasted_iota(jnp.int32, (LANES, LANES), 0) // HEAD_DIM
    col = lax.broadcasted_iota(jnp.int32, (LANES, LANES), 1) // HEAD_DIM
    return jnp.where(row == col, 1.0, 0.0).astype(BF16)


def half_turn(value):
    first = (lane_ids() & (HEAD_DIM - 1)) < HEAD_DIM // 2
    return jnp.where(
        first,
        pltpu.roll(value, LANES - HEAD_DIM // 2, 1),
        pltpu.roll(value, HEAD_DIM // 2, 1),
    )


def angles(tile, near_ref, far_ref):
    cos_r, sin_r = near_ref[0], near_ref[1]
    cos_0 = far_ref[0, pl.ds(tile, 1), :]
    sin_0 = far_ref[1, pl.ds(tile, 1), :]
    first = (lane_ids() & (HEAD_DIM - 1)) < HEAD_DIM // 2
    sine = sin_0 * cos_r + cos_0 * sin_r
    return cos_0 * cos_r - sin_0 * sin_r, jnp.where(first, -sine, sine)


def project_kernel(
    x_ref, w_ref, gain_ref, near_ref, far_ref, q_ref, k_ref, v_ref, q_rot_ref, k_rot_ref
):
    tile = pl.program_id(0)
    cosine, sine = angles(tile, near_ref, far_ref)
    ones = ones_block()
    x = x_ref[...]
    for index, used_ref, rot_ref in ((0, q_ref, q_rot_ref), (1, k_ref, k_rot_ref)):
        raw = mm(x, w_ref[index])
        for pair in range(raw.shape[1] // LANES):
            lanes = slice(pair * LANES, (pair + 1) * LANES)
            value = raw[:, lanes]
            turned = value * cosine + half_turn(value) * sine
            factor = lax.rsqrt(head_mean(turned * turned, ones) + 1e-06)
            rot_ref[:, lanes] = turned
            used_ref[:, lanes] = (turned * factor * gain_ref[:, lanes]).astype(BF16)
    v_ref[...] = mm(x, w_ref[2]).astype(BF16)


def project(x, weight, gains, near, far):
    rows, width = x.shape
    cols = weight.shape[2]
    tile = near.shape[1]
    by_row = lambda w: pl.BlockSpec((tile, w), lambda i: (i, 0))
    return pl.pallas_call(
        project_kernel,
        grid=(rows // tile,),
        in_specs=[
            by_row(width),
            whole(weight.shape, True),
            whole((1, cols)),
            whole(near.shape),
            whole(far.shape),
        ],
        out_specs=[by_row(cols)] * 5,
        out_shape=[jax.ShapeDtypeStruct((rows, cols), BF16)] * 3
        + [jax.ShapeDtypeStruct((rows, cols), F32)] * 2,
        name="project",
    )(x, weight, gains, near, far)


def key_tiles(first_row, start, wide, narrow, visit):
    full = first_row // wide

    def step(index, carry):
        visit(pl.multiple_of(index * wide, wide), wide, False)
        return carry

    lax.fori_loop(start // wide, full, step, 0)
    diagonal = (first_row // narrow) * narrow

    @pl.when(diagonal > full * wide)
    def _():
        visit(pl.multiple_of(full * wide, narrow), narrow, False)

    visit(pl.multiple_of(diagonal, narrow), narrow, True)


def attend_kernel(
    half, wide, tiles, starts, q_ref, k_ref, v_ref, w_ref, o_ref, lse_ref, send_ref, keep_ref, acc
):
    index = pl.program_id(0)
    rows = q_ref.shape[0]
    first_row = tiles[index] * rows
    start = starts[index]
    narrow = wide // 2
    low = lane_ids() < HEAD_DIM
    zero = jnp.zeros((), BF16)
    results = []
    for pair in range(q_ref.shape[1] // LANES):
        lanes = slice(pair * LANES, (pair + 1) * LANES)
        q = q_ref[:, lanes] * jnp.asarray(1.0 / math.sqrt(HEAD_DIM), BF16)
        q_both = jnp.concatenate([jnp.where(low, q, zero), jnp.where(low, zero, q)], axis=0)
        acc[...] = jnp.zeros_like(acc)

        def visit(key_0, size, masked):
            keys = pl.ds(key_0, size)
            weights = jnp.exp(mm(q_both, k_ref[keys, lanes], NT))
            if masked:
                row = lax.broadcasted_iota(jnp.int32, (2 * rows, size), 0)
                row = jnp.where(row < rows, row, row - rows) + first_row
                col = lax.broadcasted_iota(jnp.int32, (2 * rows, size), 1) + key_0
                weights = jnp.where((col <= row) & (col >= start), weights, 0.0)
            total = weights[:, :LANES]
            for part in range(1, size // LANES):
                total = total + weights[:, part * LANES : (part + 1) * LANES]
            acc[:, LANES:] += total
            acc[:, :LANES] += mm(weights.astype(BF16), v_ref[keys, lanes])

        key_tiles(first_row, start, wide, narrow, visit)
        total_a = jnp.sum(acc[:rows, LANES:], axis=1, keepdims=True)
        total_b = jnp.sum(acc[rows:, LANES:], axis=1, keepdims=True)
        summed = jnp.where(low, acc[:rows, :LANES], acc[rows:, :LANES])
        out = (summed / jnp.where(low, total_a, total_b)).astype(BF16)
        o_ref[:, lanes] = out
        lse_ref[:, lanes] = jnp.log(jnp.where(low, total_b, total_a))
        results.append(out)
    part = mm(jnp.concatenate(results, axis=1), w_ref[...]).astype(BF16)

    @pl.when(index < half)
    def _():
        send_ref[...] = part

    @pl.when(index >= half)
    def _():
        keep_ref[...] = part


def attend(q, k, v, weight, tiles, starts, rows):
    count = tiles.shape[0]
    half = count // 2
    total, cols = k.shape
    width = weight.shape[1]
    at_tile = pl.BlockSpec((rows, cols), lambda i, t, s: (t[i], 0))
    at_step = pl.BlockSpec((rows, cols), lambda i, t, s: (i, 0))
    return pl.pallas_call(
        functools.partial(attend_kernel, half, 2 * BLOCK * 2),
        grid_spec=pltpu.PrefetchScalarGridSpec(
            num_scalar_prefetch=2,
            grid=(count,),
            in_specs=[at_tile, whole(k.shape), whole(v.shape), whole(weight.shape)],
            out_specs=[
                at_step,
                at_step,
                pl.BlockSpec((rows, width), lambda i, t, s: (jnp.minimum(i, half - 1), 0)),
                pl.BlockSpec((rows, width), lambda i, t, s: (jnp.maximum(i - half, 0), 0)),
            ],
            scratch_shapes=[pltpu.VMEM((2 * rows, 2 * LANES), F32)],
        ),
        out_shape=[
            jax.ShapeDtypeStruct((count * rows, cols), BF16),
            jax.ShapeDtypeStruct((count * rows, cols), F32),
            jax.ShapeDtypeStruct((half * rows, width), BF16),
            jax.ShapeDtypeStruct((half * rows, width), BF16),
        ],
        name="attend",
    )(tiles, starts, q, k, v, weight)


def attend_back_kernel(blocks, wide, tiles, starts, *refs):
    row_refs = refs[:blocks]
    q_ref, k_ref, v_ref, o_ref, lse_ref, w_ref = refs[blocks : blocks + 6]
    dq_ref, dk_ref, dv_ref, dw_ref, rows_s, acc = refs[blocks + 6 :]
    index = pl.program_id(0)
    rows = q_ref.shape[0]
    narrow = wide // 2

    @pl.when(index == 0)
    def _():
        dk_ref[...] = jnp.zeros_like(dk_ref)
        dv_ref[...] = jnp.zeros_like(dv_ref)
        dw_ref[...] = jnp.zeros_like(dw_ref)

    for block in range(blocks):

        @pl.when(index == block)
        def _(block=block):
            rows_s[...] = row_refs[block][...]

    first_row = tiles[index] * rows
    start = starts[index]
    low = lane_ids() < HEAD_DIM
    place = lane_ids() & (HEAD_DIM - 1)
    zero = jnp.zeros((), BF16)
    ones = jnp.where(place < 3, 1.0, 0.0).astype(BF16)

    def parts(value):
        high = value.astype(BF16).astype(F32)
        rest = value - high
        middle = rest.astype(BF16).astype(F32)
        picked = jnp.where(place == 1, middle, jnp.where(place == 2, rest - middle, 0.0))
        return jnp.where(place == 0, high, picked).astype(BF16)

    d_rows = rows_s[...]
    d_attn = mm(d_rows, w_ref[...], NT).astype(BF16)
    dw_ref[...] += mm(d_rows, o_ref[...], TN)
    for pair in range(q_ref.shape[1] // LANES):
        lanes = slice(pair * LANES, (pair + 1) * LANES)
        q = q_ref[:, lanes] * jnp.asarray(1.0 / math.sqrt(HEAD_DIM), BF16)
        d_out = d_attn[:, lanes]
        minus_lse = parts(-lse_ref[:, lanes])
        product = d_out.astype(F32) * o_ref[:, lanes].astype(F32)
        sum_a = jnp.sum(jnp.where(low, product, 0.0), axis=1, keepdims=True)
        sum_b = jnp.sum(jnp.where(low, 0.0, product), axis=1, keepdims=True)
        minus_delta = parts(-jnp.where(low, sum_b, sum_a))
        q_ext = (jnp.where(low, q, minus_lse), jnp.where(low, minus_lse, q))
        d_ext = (jnp.where(low, d_out, minus_delta), jnp.where(low, minus_delta, d_out))
        q_both = jnp.concatenate([jnp.where(low, q, zero), jnp.where(low, zero, q)], axis=0)
        d_both = jnp.concatenate(
            [jnp.where(low, d_out, zero), jnp.where(low, zero, d_out)], axis=0
        )
        acc[...] = jnp.zeros_like(acc)

        def visit(key_0, size, masked):
            keys = pl.ds(key_0, size)
            k = k_ref[keys, lanes]
            v = v_ref[keys, lanes]
            k_ext = (jnp.where(low, k, ones), jnp.where(low, ones, k))
            v_ext = (jnp.where(low, v, ones), jnp.where(low, ones, v))
            if masked:
                col = lax.broadcasted_iota(jnp.int32, (size, rows), 1) + first_row
                row = lax.broadcasted_iota(jnp.int32, (size, rows), 0) + key_0
                allowed = (row <= col) & (row >= start)
            probs = []
            d_scores = []
            for head in range(2):
                prob = jnp.exp(mm(k_ext[head], q_ext[head], NT))
                if masked:
                    prob = jnp.where(allowed, prob, 0.0)
                d_score = prob * mm(v_ext[head], d_ext[head], NT)
                probs.append(prob.astype(BF16))
                d_scores.append(d_score.astype(BF16))
            dv_ref[keys, lanes] += mm(jnp.concatenate(probs, axis=1), d_both)
            dk_ref[keys, lanes] += mm(jnp.concatenate(d_scores, axis=1), q_both)
            k_both = jnp.concatenate([jnp.where(low, k, zero), jnp.where(low, zero, k)], axis=0)
            acc[...] += mm(jnp.concatenate(d_scores, axis=0), k_both, TN)

        key_tiles(first_row, start, wide, narrow, visit)
        dq_ref[:, lanes] = acc[...] * (1.0 / math.sqrt(HEAD_DIM))


def attend_back(row_blocks, q, k, v, o, lse, weight, tiles, starts, rows):
    count = tiles.shape[0]
    total, cols = k.shape
    width = weight.shape[1]
    at_tile = pl.BlockSpec((rows, cols), lambda i, t, s: (t[i], 0))
    at_step = pl.BlockSpec((rows, cols), lambda i, t, s: (i, 0))
    return pl.pallas_call(
        functools.partial(attend_back_kernel, len(row_blocks), 2 * BLOCK * 2),
        grid_spec=pltpu.PrefetchScalarGridSpec(
            num_scalar_prefetch=2,
            grid=(count,),
            in_specs=[whole(b.shape, True) for b in row_blocks]
            + [at_tile, whole(k.shape), whole(v.shape), at_step, at_step, whole(weight.shape)],
            out_specs=[at_step, whole(k.shape), whole(k.shape), whole((width, cols))],
            scratch_shapes=[pltpu.VMEM((rows, width), BF16), pltpu.VMEM((rows, LANES), F32)],
        ),
        out_shape=[
            jax.ShapeDtypeStruct((count * rows, cols), F32),
            jax.ShapeDtypeStruct((total, cols), F32),
            jax.ShapeDtypeStruct((total, cols), F32),
            jax.ShapeDtypeStruct((width, cols), F32),
        ],
        name="attend_back",
    )(tiles, starts, *row_blocks, q, k, v, o, lse, weight)


def sum_parts(refs):
    total = refs[0][...].astype(F32)
    for ref in refs[1:]:
        total = total + ref[...].astype(F32)
    return total


def join_attention_kernel(parts, place, *refs):
    x_ref, rate_ref = refs[parts : parts + 2]
    low_ref, hidden_ref, branch_ref = refs[parts + 2 :]
    branch = sum_parts(refs[:parts])
    x = x_ref[...].astype(F32)
    hidden = rms_rows(x + rate_ref[0:1] * (rms_rows(branch) - x))
    branch_ref[...] = branch
    hidden_ref[...] = hidden
    low_ref[...] = hidden.astype(BF16)


def part_specs(parts, rows, width):
    return [
        pl.BlockSpec((rows, width), lambda i, p, last=a.shape[0] // rows: (last - SUB + i, 0))
        for a in parts
    ]


SUB = 4


def join_attention(parts, x, place, rates, share):
    width = x.shape[1]
    rows = share // SUB
    here = pl.BlockSpec((rows, width), lambda i, p: (i, 0))
    return pl.pallas_call(
        functools.partial(join_attention_kernel, len(parts)),
        grid_spec=pltpu.PrefetchScalarGridSpec(
            num_scalar_prefetch=1,
            grid=(SUB,),
            in_specs=part_specs(parts, rows, width)
            + [pl.BlockSpec((rows, width), lambda i, p: (p[0] * SUB + i, 0)), whole(rates.shape)],
            out_specs=[here] * 3,
        ),
        out_shape=[
            jax.ShapeDtypeStruct((share, width), BF16),
            jax.ShapeDtypeStruct((share, width), F32),
            jax.ShapeDtypeStruct((share, width), F32),
        ],
        name="join_attention",
    )(place, *parts, x, rates)


def mlp_kernel(blocks, *refs):
    row_refs = refs[:blocks]
    w_ref, down_ref, scale_ref = refs[blocks : blocks + 3]
    full_ref, up_ref, gate_ref, mixed_ref, send_ref, keep_ref = refs[blocks + 3 :]
    index = pl.program_id(0)
    half = blocks // 2
    rows = row_refs[0].shape[0]
    for side in range(2):

        @pl.when(index == side)
        def _(side=side):
            for block in range(half):
                full_ref[block * rows : (block + 1) * rows] = row_refs[side * half + block][...]

    x = full_ref[...]
    cols = w_ref.shape[2]
    step = 2 * BLOCK
    for col in range(0, cols, step):
        lanes = slice(col, col + step)
        up = mm(x, w_ref[0, :, lanes])
        gate = mm(x, w_ref[1, :, lanes])
        up_ref[:, lanes] = up.astype(BF16)
        gate_ref[:, lanes] = gate.astype(BF16)
        scaled = gate * scale_ref[1:2, lanes]
        mixed_ref[:, lanes] = (
            up * scale_ref[0:1, lanes] * (scaled * jax.nn.sigmoid(scaled))
        ).astype(BF16)
    part = mm(mixed_ref[...], down_ref[...]).astype(BF16)

    @pl.when(index == 0)
    def _():
        send_ref[...] = part

    @pl.when(index == 1)
    def _():
        keep_ref[...] = part


def mlp(row_blocks, weight, down, scale):
    rows, width = row_blocks[0].shape
    side = rows * len(row_blocks) // 2
    cols = weight.shape[2]
    at_step = lambda w: pl.BlockSpec((side, w), lambda i: (i, 0))
    return pl.pallas_call(
        functools.partial(mlp_kernel, len(row_blocks)),
        grid=(2,),
        in_specs=[whole(b.shape, True) for b in row_blocks]
        + [whole(weight.shape, True), whole(down.shape, True), whole(scale.shape)],
        out_specs=[at_step(width), at_step(cols), at_step(cols), at_step(cols)]
        + [whole((side, width))] * 2,
        out_shape=[jax.ShapeDtypeStruct((2 * side, width), BF16)]
        + [jax.ShapeDtypeStruct((2 * side, cols), BF16)] * 3
        + [jax.ShapeDtypeStruct((side, width), BF16)] * 2,
        name="mlp",
    )(*row_blocks, weight, down, scale)


def join_mlp_kernel(parts, *refs):
    hidden_ref, cot_ref, rate_ref = refs[parts : parts + 3]
    out_ref, low_ref, d_hidden_ref, rate_grad_ref = refs[parts + 3 :]
    branch = sum_parts(refs[:parts])
    hidden = hidden_ref[...]
    rate = rate_ref[1:2]
    factor = rms_factor(branch)
    normed = branch * factor
    gap = normed - hidden
    before = hidden + rate * gap
    factor_out = rms_factor(before)
    out = before * factor_out
    d_before = rms_back(out, factor_out, cot_ref[...].astype(F32))
    out_ref[...] = out
    d_hidden_ref[...] = (1.0 - rate) * d_before
    low_ref[...] = rms_back(normed, factor, rate * d_before).astype(BF16)

    @pl.when(pl.program_id(0) == 0)
    def _():
        rate_grad_ref[...] = jnp.zeros_like(rate_grad_ref)

    rate_grad_ref[...] += jnp.sum(d_before * gap, axis=0, keepdims=True)


def join_mlp(parts, hidden, cotangent, chunk, rates, share):
    width = hidden.shape[1]
    rows = share // SUB
    here = pl.BlockSpec((rows, width), lambda i, p: (i, 0))
    return pl.pallas_call(
        lambda p, *refs: join_mlp_kernel(len(parts), *refs),
        grid_spec=pltpu.PrefetchScalarGridSpec(
            num_scalar_prefetch=1,
            grid=(SUB,),
            in_specs=part_specs(parts, rows, width)
            + [
                here,
                pl.BlockSpec((rows, width), lambda i, p: (chunk * SUB + i, 0)),
                whole(rates.shape),
            ],
            out_specs=[here] * 3 + [whole((1, width))],
        ),
        out_shape=[
            jax.ShapeDtypeStruct((share, width), F32),
            jax.ShapeDtypeStruct((share, width), BF16),
            jax.ShapeDtypeStruct((share, width), F32),
            jax.ShapeDtypeStruct((1, width), F32),
        ],
        name="join_mlp",
    )(jnp.zeros((1,), jnp.int32), *parts, hidden, cotangent, rates)


def mlp_back_kernel(blocks, *refs):
    row_refs = refs[:blocks]
    up_ref, gate_ref, w_ref, down_ref, scale_ref = refs[blocks : blocks + 5]
    full_ref, d_up_ref, d_gate_ref, sums_ref, send_ref, keep_ref = refs[blocks + 5 :]
    index = pl.program_id(0)
    half = blocks // 2
    rows = row_refs[0].shape[0]
    for side in range(2):

        @pl.when(index == side)
        def _(side=side):
            for block in range(half):
                full_ref[block * rows : (block + 1) * rows] = row_refs[side * half + block][...]

    @pl.when(index == 0)
    def _():
        sums_ref[...] = jnp.zeros_like(sums_ref)

    d_rows = full_ref[...]
    cols = w_ref.shape[2]
    step = 2 * BLOCK
    for col in range(0, cols, step):
        lanes = slice(col, col + step)
        d_mixed = mm(d_rows, down_ref[lanes, :], NT)
        up_raw = up_ref[:, lanes].astype(F32)
        gate_raw = gate_ref[:, lanes].astype(F32)
        scale_up = scale_ref[0:1, lanes]
        scale_gate = scale_ref[1:2, lanes]
        gate = gate_raw * scale_gate
        sig = jax.nn.sigmoid(gate)
        d_up = d_mixed * (gate * sig)
        d_gate = d_mixed * (up_raw * scale_up) * (sig * (1.0 + gate * (1.0 - sig)))
        sums_ref[0:1, lanes] += jnp.sum(d_up * up_raw, axis=0, keepdims=True)
        sums_ref[1:2, lanes] += jnp.sum(d_gate * gate_raw, axis=0, keepdims=True)
        d_up_ref[:, lanes] = (d_up * scale_up).astype(BF16)
        d_gate_ref[:, lanes] = (d_gate * scale_gate).astype(BF16)
    part = (mm(d_up_ref[...], w_ref[0], NT) + mm(d_gate_ref[...], w_ref[1], NT)).astype(BF16)

    @pl.when(index == 0)
    def _():
        send_ref[...] = part

    @pl.when(index == 1)
    def _():
        keep_ref[...] = part


def mlp_back(row_blocks, up, gate, weight, down, scale):
    rows, width = row_blocks[0].shape
    side = rows * len(row_blocks) // 2
    cols = weight.shape[2]
    at_step = lambda w: pl.BlockSpec((side, w), lambda i: (i, 0))
    return pl.pallas_call(
        functools.partial(mlp_back_kernel, len(row_blocks)),
        grid=(2,),
        in_specs=[whole(b.shape, True) for b in row_blocks]
        + [
            at_step(cols),
            at_step(cols),
            whole(weight.shape, True),
            whole(down.shape, True),
            whole(scale.shape),
        ],
        out_specs=[at_step(width), at_step(cols), at_step(cols), whole(scale.shape)]
        + [whole((side, width))] * 2,
        out_shape=[jax.ShapeDtypeStruct((2 * side, width), BF16)]
        + [jax.ShapeDtypeStruct((2 * side, cols), BF16)] * 2
        + [jax.ShapeDtypeStruct(scale.shape, F32)]
        + [jax.ShapeDtypeStruct((side, width), BF16)] * 2,
        name="mlp_back",
    )(*row_blocks, up, gate, weight, down, scale)


def split_attention_kernel(parts, place, *refs):
    d_hidden_ref, hidden_ref, branch_ref, x_ref, rate_ref = refs[parts : parts + 5]
    low_ref, d_input_ref, rate_grad_ref = refs[parts + 5 :]
    d_hidden = sum_parts(refs[:parts]) + d_hidden_ref[...]
    hidden = hidden_ref[...]
    branch = branch_ref[...]
    x = x_ref[...].astype(F32)
    rate = rate_ref[0:1]
    factor = rms_factor(branch)
    normed = branch * factor
    gap = normed - x
    d_before = rms_back(hidden, rms_factor(x + rate * gap), d_hidden)
    d_input_ref[...] = (1.0 - rate) * d_before
    low_ref[...] = rms_back(normed, factor, rate * d_before).astype(BF16)

    @pl.when(pl.program_id(0) == 0)
    def _():
        rate_grad_ref[...] = jnp.zeros_like(rate_grad_ref)

    rate_grad_ref[...] += jnp.sum(d_before * gap, axis=0, keepdims=True)


def split_attention(parts, d_hidden, hidden, branch, x, place, rates, share):
    width = x.shape[1]
    rows = share // SUB
    here = pl.BlockSpec((rows, width), lambda i, p: (i, 0))
    return pl.pallas_call(
        functools.partial(split_attention_kernel, len(parts)),
        grid_spec=pltpu.PrefetchScalarGridSpec(
            num_scalar_prefetch=1,
            grid=(SUB,),
            in_specs=part_specs(parts, rows, width)
            + [here] * 3
            + [pl.BlockSpec((rows, width), lambda i, p: (p[0] * SUB + i, 0)), whole(rates.shape)],
            out_specs=[here] * 2 + [whole((1, width))],
        ),
        out_shape=[
            jax.ShapeDtypeStruct((share, width), BF16),
            jax.ShapeDtypeStruct((share, width), F32),
            jax.ShapeDtypeStruct((1, width), F32),
        ],
        name="split_attention",
    )(place, *parts, d_hidden, hidden, branch, x, rates)


def project_back_kernel(order, *refs):
    (
        x_ref,
        q_rot_ref,
        k_rot_ref,
        w_ref,
        gain_ref,
        near_ref,
        far_ref,
    ) = refs[:7]
    dq_refs = refs[7 : 7 + CHUNKS]
    dk_refs = refs[7 + CHUNKS : 7 + 2 * CHUNKS]
    dv_refs = refs[7 + 2 * CHUNKS : 7 + 3 * CHUNKS]
    send_ref, keep_ref, gain_grad_ref, grad_ref, acc = refs[7 + 3 * CHUNKS :]
    index = pl.program_id(0)
    count = pl.num_programs(0)

    @pl.when(index == 0)
    def _():
        gain_grad_ref[...] = jnp.zeros_like(gain_grad_ref)
        acc[...] = jnp.zeros_like(acc)

    tile = order[index]
    cosine, sine = angles(tile, near_ref, far_ref)
    ones = ones_block()
    cols = q_rot_ref.shape[1]
    chunk = index % CHUNKS
    dq = dq_refs[0][...]
    for other in range(1, CHUNKS):
        dq = jnp.where(chunk == other, dq_refs[other][...], dq)
    d_raw = []
    for used, rot_ref in ((dq, q_rot_ref), (sum_parts(dk_refs), k_rot_ref)):
        for pair in range(cols // LANES):
            lanes = slice(pair * LANES, (pair + 1) * LANES)
            turned = rot_ref[:, lanes]
            factor = lax.rsqrt(head_mean(turned * turned, ones) + 1e-06)
            normed = turned * factor
            d_used = used[:, lanes]
            gain_grad_ref[:, lanes] += jnp.sum(d_used * normed, axis=0, keepdims=True)
            d_normed = d_used * gain_ref[:, lanes]
            d_turned = factor * (d_normed - normed * head_mean(d_normed * normed, ones))
            d_raw.append((d_turned * cosine - half_turn(d_turned) * sine).astype(BF16))
    d_raw.append(sum_parts(dv_refs).astype(BF16))
    d_all = jnp.concatenate(d_raw, axis=1)
    part = mm(d_all[:, :cols], w_ref[0], NT)
    part = part + mm(d_all[:, cols : 2 * cols], w_ref[1], NT)
    part = (part + mm(d_all[:, 2 * cols :], w_ref[2], NT)).astype(BF16)
    acc[...] += mm(x_ref[...], d_all, TN)

    @pl.when(index < count // 2)
    def _():
        send_ref[...] = part

    @pl.when(index >= count // 2)
    def _():
        keep_ref[...] = part

    @pl.when(index == count - 1)
    def _():
        grad_ref[...] = acc[...].astype(BF16)


def project_back(x, q_rot, k_rot, weight, gains, near, far, dq, dk, dv, order, rows):
    total, width = x.shape
    cols = weight.shape[2]
    count = order.shape[0]
    half = count // 2
    at_tile = lambda w: pl.BlockSpec((rows, w), lambda i, t: (t[i], 0))
    return pl.pallas_call(
        project_back_kernel,
        grid_spec=pltpu.PrefetchScalarGridSpec(
            num_scalar_prefetch=1,
            grid=(count,),
            in_specs=[
                at_tile(width),
                at_tile(cols),
                at_tile(cols),
                whole(weight.shape, True),
                whole((1, cols)),
                whole(near.shape),
                whole(far.shape),
            ]
            + [pl.BlockSpec((rows, cols), lambda i, t: (i // CHUNKS, 0))] * CHUNKS
            + [at_tile(cols)] * (2 * CHUNKS),
            out_specs=[
                pl.BlockSpec((rows, width), lambda i, t: (jnp.minimum(i, half - 1), 0)),
                pl.BlockSpec((rows, width), lambda i, t: (jnp.maximum(i - half, 0), 0)),
                whole((1, cols)),
                whole((width, 3 * cols)),
            ],
            scratch_shapes=[pltpu.VMEM((width, 3 * cols), F32)],
        ),
        out_shape=[
            jax.ShapeDtypeStruct((half * rows, width), BF16),
            jax.ShapeDtypeStruct((half * rows, width), BF16),
            jax.ShapeDtypeStruct((1, cols), F32),
            jax.ShapeDtypeStruct((width, 3 * cols), BF16),
        ],
        name="project_back",
    )(order, x, q_rot, k_rot, weight, gains, near, far, *dq, *dk, *dv)


def outer_kernel(chunks, *refs):
    left_refs = refs[:chunks]
    right_refs = refs[chunks : 2 * chunks]
    out_ref = refs[2 * chunks]
    total = mm(left_refs[0][...], right_refs[0][...], TN)
    for left, right in zip(left_refs[1:], right_refs[1:], strict=True):
        total = total + mm(left[...], right[...], TN)
    out_ref[...] = total.astype(BF16)


def outer(left, right, step):
    rows, width = left[0].shape
    cols = right[0].shape[1]
    return pl.pallas_call(
        functools.partial(outer_kernel, len(left)),
        grid=(cols // step,),
        in_specs=[whole((rows, width), True)] * len(left)
        + [pl.BlockSpec((rows, step), lambda i: (0, i))] * len(right),
        out_specs=pl.BlockSpec((width, step), lambda i: (0, i)),
        out_shape=jax.ShapeDtypeStruct((width, cols), BF16),
        name="outer",
    )(*left, *right)


def two_parts(value):
    high = value.astype(BF16)
    return high, (value - high.astype(F32)).astype(BF16)


def step_kernel(g_ref, left_ref, right_ref, master_ref, grad_ref, stepped_ref, square_ref):
    owners, slots, piece, width = g_ref.shape
    for slot in range(slots):
        low = jnp.concatenate([g_ref[o, slot] for o in range(owners)], axis=0)
        grad_ref[slot] = low.astype(F32)
        high, rest = two_parts(left_ref[slot])
        turned = mm(high, low) + mm(rest, low)
        t_high, t_rest = two_parts(turned)
        r_high, r_rest = two_parts(right_ref[slot])
        direction = mm(t_high, r_high) + mm(t_high, r_rest) + mm(t_rest, r_high)
        stepped = master_ref[slot] - 0.3 * direction
        stepped_ref[slot] = stepped
        square_ref[slot : slot + 1] = jnp.sum(stepped * stepped, axis=0, keepdims=True)


def stats_kernel(g_ref, left_ref, right_ref, new_left_ref, new_right_ref):
    owners, slots, piece, width = g_ref.shape
    for slot in range(slots):
        low = jnp.concatenate([g_ref[o, slot] for o in range(owners)], axis=0)
        new_left_ref[slot] = 0.5 * left_ref[slot] + 0.5 * mm(low, low, NT)
        new_right_ref[slot] = 0.5 * right_ref[slot] + 0.5 * mm(low, low, TN)


def finish_kernel(stepped_ref, ema_ref, norm_ref, master_ref, new_ema_ref):
    slots = stepped_ref.shape[0]
    for slot in range(slots):
        master = stepped_ref[slot] * lax.rsqrt(norm_ref[slot : slot + 1] + 1e-06)
        master_ref[slot] = master
        new_ema_ref[slot] = 0.5 * ema_ref[slot] + 0.5 * master


def block_specs(count, slots):
    return pl.BlockSpec((slots, BLOCK, BLOCK), lambda i: (i, 0, 0))


def exchange(value, axis, pairs):
    return lax.ppermute(value, axis, pairs)


def shards(
    tokens,
    seq_lengths,
    qkv_weight,
    out_weight,
    up_gate_weight,
    down_weight,
    qk_scale,
    mlp_scale,
    eigen_rates,
    cotangent,
    block_order,
    master_blocks,
    ema_blocks,
    left_stats,
    right_stats,
    left_root,
    right_root,
):
    x_rows = tokens[0]
    total, width = x_rows.shape
    cols = qk_scale.shape[0]
    heads = lax.axis_size("head")
    owners = lax.axis_size("batch")
    ranks = heads // 2
    here = lax.axis_index("head")
    rank, core = here // 2, here % 2
    share = total // heads
    rows = share // CHUNKS
    tiles_all = total // rows

    core_swap = [(i, i ^ 1) for i in range(heads)]
    shift_up = [
        [(i, (i // 2 + s) % ranks * 2 + i % 2) for i in range(heads)] for s in range(ranks)
    ]
    shift_down = [
        [(i, (i // 2 - s) % ranks * 2 + i % 2) for i in range(heads)] for s in range(ranks)
    ]
    far_steps = list(range(1, ranks))
    ring = far_steps + [0]

    shares = jnp.stack(
        [(rank - s) % ranks * 2 + (core + d) % 2 for d in (1, 0) for s in ring]
    ).astype(jnp.int32)
    ends = jnp.cumsum(seq_lengths[0])

    def begin_of(row):
        segment = jnp.sum((row[:, None] >= ends[None, :]).astype(jnp.int32), axis=1)
        member = segment[:, None] == jnp.arange(ends.shape[0], dtype=jnp.int32)[None, :]
        return jnp.sum(jnp.where(member, (ends - seq_lengths[0])[None, :], 0), axis=1)

    tile_rows = jnp.arange(tiles_all, dtype=jnp.int32) * rows
    tile_begin = begin_of(tile_rows)
    lane = jnp.arange(LANES, dtype=jnp.int32) % (HEAD_DIM // 2)
    freq = 10000.0 ** (-lane.astype(F32) * 2.0 / HEAD_DIM)
    near_angle = jnp.arange(rows, dtype=F32)[:, None] * freq[None, :]
    far_angle = (tile_rows - tile_begin).astype(F32)[:, None] * freq[None, :]
    near = jnp.stack([jnp.cos(near_angle), jnp.sin(near_angle)])
    far = jnp.stack([jnp.cos(far_angle), jnp.sin(far_angle)])
    gains = qk_scale[None, :]
    rates = eigen_rates.T

    q, k, v, q_rot, k_rot = project(x_rows, qkv_weight, gains, near, far)

    def reduce_to_shares(send, keep, size):
        got = exchange(send, "head", core_swap)
        parts = [keep, got]
        if ranks > 1:
            away = (keep[: -size].astype(F32) + got[: -size].astype(F32)).astype(BF16)
            for n, s in enumerate(far_steps):
                parts.append(
                    exchange(away[n * size : (n + 1) * size], "head", shift_down[s])
                )
        return parts

    def gather_shares(own):
        mine = [exchange(own, "head", shift_up[s]) for s in far_steps] + [own]
        return [exchange(b, "head", core_swap) for b in mine] + mine

    places = [(here * CHUNKS + j).astype(jnp.int32)[None] for j in range(CHUNKS)]
    tiles = [shares * CHUNKS + j for j in range(CHUNKS)]
    starts = [begin_of(t * rows) for t in tiles]
    chunks = range(CHUNKS)
    fwd = [attend(q, k, v, out_weight, tiles[j], starts[j], rows) for j in chunks]
    attn_out = [f[0] for f in fwd]
    lse = [f[1] for f in fwd]
    joined = []
    for j in chunks:
        parts = reduce_to_shares(fwd[j][2], fwd[j][3], rows)
        joined.append(join_attention(parts, x_rows, places[j], rates, rows))
    ffn = [
        mlp(gather_shares(joined[j][0]), up_gate_weight, down_weight, mlp_scale) for j in chunks
    ]
    ends_fwd = []
    for j in chunks:
        parts = reduce_to_shares(ffn[j][4], ffn[j][5], rows)
        ends_fwd.append(join_mlp(parts, joined[j][1], cotangent[0], j, rates, rows))
    back = [
        mlp_back(
            gather_shares(ends_fwd[j][1]),
            ffn[j][1],
            ffn[j][2],
            up_gate_weight,
            down_weight,
            mlp_scale,
        )
        for j in chunks
    ]
    split = []
    for j in chunks:
        parts = reduce_to_shares(back[j][4], back[j][5], rows)
        split.append(
            split_attention(
                parts,
                ends_fwd[j][2],
                joined[j][1],
                joined[j][2],
                x_rows,
                places[j],
                rates,
                rows,
            )
        )
    hidden_full = [ffn[j][0] for j in chunks]
    d_mlp_rows = [back[j][0] for j in chunks]
    grad_up = outer(hidden_full, [back[j][1] for j in chunks], 2 * BLOCK)
    grad_gate = outer(hidden_full, [back[j][2] for j in chunks], 2 * BLOCK)
    grad_down = outer(d_mlp_rows, [ffn[j][3] for j in chunks], 2 * BLOCK)
    attn_back = [
        attend_back(
            gather_shares(split[j][0]),
            q,
            k,
            v,
            attn_out[j],
            lse[j],
            out_weight,
            tiles[j],
            starts[j],
            rows,
        )
        for j in chunks
    ]
    order = (shares[:, None] * CHUNKS + jnp.arange(CHUNKS, dtype=jnp.int32)[None, :]).reshape(-1)
    send, keep, gain_grad, grad_qkv = project_back(
        x_rows,
        q_rot,
        k_rot,
        qkv_weight,
        gains,
        near,
        far,
        [a[0] for a in attn_back],
        [a[1] for a in attn_back],
        [a[2] for a in attn_back],
        order,
        rows,
    )
    parts = reduce_to_shares(send, keep, share)
    d_input = jnp.concatenate([s[1] for s in split], axis=0)
    d_input = d_input + sum(p[-share:].astype(F32) for p in parts)

    def double(value, axis, size):
        step = 1
        while step < size:
            value = value + exchange(value, axis, [(i, i ^ step) for i in range(size)])
            step *= 2
        return value

    rate_grad = jnp.concatenate(
        [sum(s[2] for s in split), sum(e[3] for e in ends_fwd)], axis=0
    )
    rate_grad = double(rate_grad, "head", heads)
    scale_grad = sum(b[3] for b in back)
    small = double(
        jnp.concatenate([rate_grad.reshape(-1), scale_grad.reshape(-1)]), "batch", owners
    )
    gain_sum = double(gain_grad[0], "batch", owners)
    rate_sum = small[: 2 * width].reshape(2, width)
    scale_sum = small[2 * width :].reshape(mlp_scale.shape)

    row_blocks = width // BLOCK
    piece = BLOCK // owners

    def as_pieces(matrix):
        panels = matrix.shape[1] // BLOCK
        return (
            matrix.reshape(row_blocks, owners, piece, panels, BLOCK)
            .transpose(1, 3, 0, 2, 4)
            .reshape(owners, panels * row_blocks * piece, BLOCK)
        )

    def summed(matrix):
        return lax.psum_scatter(
            as_pieces(matrix), "batch", scatter_dimension=0, tiled=False
        ).reshape(-1, piece, BLOCK)

    grad_out = sum(a[3] for a in attn_back).astype(BF16)
    late = summed(jnp.concatenate([grad_qkv, grad_out], axis=1))
    early = summed(jnp.concatenate([grad_up, grad_gate, grad_down], axis=1))
    pieces = jnp.concatenate([late, early], axis=0)
    slot_order = block_order[0]
    ordered = jnp.take(pieces, slot_order, axis=0)
    per_owner = ordered.shape[0] // owners
    owned = lax.all_to_all(
        ordered.reshape(owners, per_owner, piece, BLOCK),
        "batch",
        split_axis=0,
        concat_axis=0,
        tiled=True,
    )
    slots = min(8, per_owner)
    if piece % 16:
        owned = owned.transpose(1, 0, 2, 3).reshape(1, per_owner, BLOCK, BLOCK)
    g_spec = pl.BlockSpec(
        (owned.shape[0], slots) + owned.shape[2:], lambda i: (0, i, 0, 0)
    )
    blk = pl.BlockSpec((slots, BLOCK, BLOCK), lambda i: (i, 0, 0))
    row = pl.BlockSpec((slots, BLOCK), lambda i: (i, 0))
    cube = jax.ShapeDtypeStruct((per_owner, BLOCK, BLOCK), F32)
    grid = (per_owner // slots,)
    owned_grad, stepped, column_sq = pl.pallas_call(
        step_kernel,
        grid=grid,
        in_specs=[g_spec, blk, blk, blk],
        out_specs=[blk, blk, row],
        out_shape=[cube, cube, jax.ShapeDtypeStruct((per_owner, BLOCK), F32)],
        name="step",
    )(owned, left_root[0], right_root[0], master_blocks[0])
    new_left, new_right = pl.pallas_call(
        stats_kernel,
        grid=grid,
        in_specs=[g_spec, blk, blk],
        out_specs=[blk, blk],
        out_shape=[cube, cube],
        name="stats",
    )(owned, left_stats[0], right_stats[0])
    panels = block_order.shape[1] // row_blocks
    my_blocks = lax.dynamic_slice_in_dim(
        slot_order, lax.axis_index("batch") * per_owner, per_owner, 0
    )
    member = (
        (my_blocks // row_blocks)[:, None] == jnp.arange(panels, dtype=jnp.int32)[None, :]
    ).astype(F32)
    precise = lax.Precision.HIGHEST
    totals = double(jnp.einsum("sp,sb->pb", member, column_sq, precision=precise), "batch", owners)
    norms = jnp.einsum("sp,pb->sb", member, totals, precision=precise)
    new_master, new_ema = pl.pallas_call(
        finish_kernel,
        grid=grid,
        in_specs=[blk, blk, row],
        out_specs=[blk, blk],
        out_shape=[cube, cube],
        name="finish",
    )(stepped, ema_blocks[0], norms)
    gain_step = 0.5 / math.sqrt(total * owners)
    width_share = width // heads
    rate_here = lax.dynamic_slice_in_dim(rate_sum, here * width_share, width_share, 1)
    rate_slice = lax.dynamic_slice_in_dim(rates, here * width_share, width_share, 1)
    mlp_scale_out = jnp.stack([scale_sum, mlp_scale - gain_step * scale_sum])
    new_gains = jnp.concatenate(
        [(qk_scale - gain_step * gain_sum)[None, :], rate_slice - gain_step * rate_here], axis=0
    )
    out_share = jnp.concatenate([e[0] for e in ends_fwd], axis=0)
    return (
        out_share[None],
        d_input[None],
        owned_grad[None],
        new_master[None],
        new_ema[None],
        new_left[None],
        new_right[None],
        gain_sum,
        mlp_scale_out,
        rate_here.T,
        new_gains,
    )


def solution(mesh):
    return jax.shard_map(
        shards,
        mesh=mesh,
        in_specs=(
            P("batch", None, None),
            P("batch", None),
            P(None, None, "head"),
            P("head", None),
            P(None, None, "head"),
            P("head", None),
            P("head"),
            P(None, "head"),
            P(),
            P("batch", "head", None),
            P("head", None),
            P("head", "batch", None, None),
            P("head", "batch", None, None),
            P("head", "batch", None, None),
            P("head", "batch", None, None),
            P("head", "batch", None, None),
            P("head", "batch", None, None),
        ),
        out_specs=(
            P("batch", "head", None),
            P("batch", "head", None),
            P("head", "batch", None, None),
            P("head", "batch", None, None),
            P("head", "batch", None, None),
            P("head", "batch", None, None),
            P("head", "batch", None, None),
            P("head"),
            P(None, None, "head"),
            P("head", None),
            P(None, "head"),
        ),
        check_vma=False,
    )
```

time: 1120 us -> 638 us (0.57)
  matrix products: 331 us -> 1.78 us
  Pallas kernels: 0 us -> 218 us
  waiting for transfers between devices: 424 us -> 283 us
  other arithmetic: 153 us -> 36.5 us
  local copies, waits for them, and re-layouts: 132 us -> 22.3 us
  starting transfers between devices: 4.32 us -> 51.2 us
  blocking collectives: 37.1 us -> 0 us
  loops' own time: 16.2 us -> 0 us
    dot_general x45 -> x1, matrix products: 331 us -> 0.98 us  [shards(): jnp.einsum('sp,sb->pb', member, column_sq, precision=precise)]
    pallas_call x0 -> x22, Pallas kernels: none -> 218 us  [the longest x2 32.4 us: mlp_back(): pl.pallas_call(functools.partial(mlp_back_kernel, len(row_blocks)), grid=...]
    reduce_scatter x5 -> x2, waiting for transfers between devices: 322 us -> 178 us  [summed(): lax.psum_scatter(as_pieces(matrix), 'batch', scatter_dimension=0, tiled=F...]
    ppermute x0 -> x43, waiting for transfers between devices: none -> 106 us  [exchange(): return lax.ppermute(value, axis, pairs)]
    all_gather x3 -> x0, waiting for transfers between devices: 83.6 us -> none  [the longest x1 34.6 us: shards(): d_mlp_rows = lax.all_gather(d_branch_mlp, 'head', axis=0, tiled=True)]
    convert_element_type x11 -> x9, other arithmetic: 70.2 us -> 11.9 us  [the longest x7 10.6 us: reduce_to_shares(): away = (keep[:-size].astype(F32) + got[:-size].astype(F32)).astype(BF16)]
    reduce_sum x17 -> x4, other arithmetic: 50.1 us -> 1.18 us  [the longest x2 0.88 us: begin_of(): jnp.sum(jnp.where(member, (ends - seq_lengths[0])[None, :], 0), axis=1)]
    ppermute x0 -> x43, starting transfers between devices: none -> 47.3 us  [exchange(): return lax.ppermute(value, axis, pairs)]
  transfers between devices with their start and end apart: 10 -> 46, of which waited for: 9 -> 24; matrix products, arithmetic and copies ran while one was open for 3% -> 6% of each run, Pallas kernels for 0% -> 25%
where the time goes in v1:
time: 638 us; the launch traced here: 628 us
  waiting for transfers between devices  283 us (44%)
  Pallas kernels  218 us (34%)
  starting transfers between devices  51.2 us (8%)
  other arithmetic  36.5 us (6%)
  local copies, waits for them, and re-layouts  22.3 us (3%)
  between operations  15.1 us (2%)
    reduce_scatter x2, waiting for transfers between devices, summed(): lax.psum_scatter(as_pieces(matrix), 'batch', scatter_dimension=0, tiled=F...  178 us
    ppermute x43, waiting for transfers between devices, exchange(): return lax.ppermute(value, axis, pairs)  106 us
    ppermute x43, starting transfers between devices, exchange(): return lax.ppermute(value, axis, pairs)  47.3 us
    pallas_call x2, Pallas kernels, mlp_back(): pl.pallas_call(functools.partial(mlp_back_kernel, len(row_blocks)), grid=...  32.4 us
    pallas_call x2, Pallas kernels, attend_back(): pl.pallas_call(functools.partial(attend_back_kernel, len(row_blocks), 2 *...  32.1 us
    pallas_call x2, Pallas kernels, mlp(): pl.pallas_call(functools.partial(mlp_kernel, len(row_blocks)), grid=(2,),...  27.1 us
    pallas_call x3, Pallas kernels, outer(): pl.pallas_call(functools.partial(outer_kernel, len(left)), grid=(cols //...  27 us
    pallas_call x2, Pallas kernels, attend(): pl.pallas_call(functools.partial(attend_kernel, half, 2 * BLOCK * 2), gri...  19.9 us
  transfers between devices with their start and end apart: 46, of which 24 were waited for; matrix products, arithmetic and copies ran while one was open for 6% of the time, Pallas kernels for 25%

profile of v1, /device:TPU:0, one launch (start us, length us, event | category | flops | bytes accessed | tf_op | source)
XLA Modules:
  0.0 628.0 jit_solution(10322467630042420680)
XLA Ops:
  13.2 12.8 %project.1 = (bf16[2048,256]{1,0:T(8,128)(2,1)}, bf16[2048,256]{1,0:T(8,128)(2,1)}, bf16[2048,256]{1,0:T(8,128)(2,1)}, f32[2048,256]{1,0:T(8,128)}, f32[2048,256]{1,0:T(8,128)}) custom-call(bf16[2048,1024]{1,0:T(8,128)(2,1)} %bitcast.74, bf16[3,1024,256]{2,1,0:T(8,128)(2,1)} %refs_3_.1, f32[1,256]{1,0:T(1,128)} %bitcast.101, ...), custom_call_target="tpu_custom_call" | custom-call | tf_op jit(solution)/shard_map/project/pallas_call | solution.py:103
  25.9 11.6 %attend.3 = (bf16[1024,256]{1,0:T(8,128)(2,1)}, f32[1024,256]{1,0:T(8,128)}, bf16[512,1024]{1,0:T(8,128)(2,1)}, bf16[512,1024]{1,0:T(8,128)(2,1)}) custom-call(s32[4]{0:T(128)} %get-tuple-element.181.tiles, s32[4]{0:T(128)} %get-tuple-element.164.starts, bf16[2048,256]{1,0:T(8,128)(2,1)} %get-tuple-element.87.q_ref.refs_4_, ...), custom_call_target="tpu_custom_call" | custom-call | tf_op jit(solution)/shard_map/attend/pallas_call | solution.py:194
  38.0 8.3 %attend.2 = (bf16[1024,256]{1,0:T(8,128)(2,1)}, f32[1024,256]{1,0:T(8,128)}, bf16[512,1024]{1,0:T(8,128)(2,1)}, bf16[512,1024]{1,0:T(8,128)(2,1)}) custom-call(s32[4]{0:T(128)} %get-tuple-element.169.tiles, s32[4]{0:T(128)} %get-tuple-element.163.starts, bf16[2048,256]{1,0:T(8,128)(2,1)} %get-tuple-element.87.q_ref.refs_4_, ...), custom_call_target="tpu_custom_call" | custom-call | tf_op jit(solution)/shard_map/attend/pallas_call | solution.py:194
  53.6 10.1 %collective-permute-done.8.refs_2_ = bf16[256,1024]{1,0:T(8,128)(2,1)} collective-permute-done((bf16[256,1024]{1,0:T(8,128)(2,1)}, bf16[256,1024]{1,0:T(8,128)(2,1)}, u32[]{:S(2)}, u32[]{:S(2)}) %collective-permute-start.8) | collective-permute-done | bytes 524320 | tf_op jit(solution)/shard_map/ppermute | solution.py:769
  86.5 10.2 %collective-permute-done.2.refs_2_ = bf16[256,1024]{1,0:T(8,128)(2,1)S(1)} collective-permute-done((bf16[256,1024]{1,0:T(8,128)(2,1)}, bf16[256,1024]{1,0:T(8,128)(2,1)S(1)}, u32[]{:S(2)}, u32[]{:S(2)}) %collective-permute-start.2) | collective-permute-done | bytes 524320 | tf_op jit(solution)/shard_map/ppermute | solution.py:769
  98.3 13.3 %mlp.3 = (bf16[1024,1024]{1,0:T(8,128)(2,1)}, bf16[1024,1024]{1,0:T(8,128)(2,1)}, bf16[1024,1024]{1,0:T(8,128)(2,1)}, bf16[1024,1024]{1,0:T(8,128)(2,1)}, bf16[5...) custom-call(bf16[256,1024]{1,0:T(8,128)(2,1)} %copy-done.20, bf16[256,1024]{1,0:T(8,128)(2,1)} %copy-done.18, ...), custom_call_target="tpu_custom_call" | custom-call | tf_op jit(solution)/shard_map/mlp/pallas_call | solution.py:419
  112.9 13.8 %mlp.2 = (bf16[1024,1024]{1,0:T(8,128)(2,1)}, bf16[1024,1024]{1,0:T(8,128)(2,1)}, bf16[1024,1024]{1,0:T(8,128)(2,1)}, bf16[1024,1024]{1,0:T(8,128)(2,1)}, bf16[5...) custom-call(bf16[256,1024]{1,0:T(8,128)(2,1)} %collective-permute-done.3.refs_0_, bf16[256,1024]{1,0:T(8,128)(2,1)} %copy-done.16, ...), custom_call_target="tpu_custom_call" | custom-call | tf_op jit(solution)/shard_map/mlp/pallas_call | solution.py:419
  133.9 8.1 %collective-permute-done.13.refs_2_ = bf16[256,1024]{1,0:T(8,128)(2,1)S(1)} collective-permute-done((bf16[256,1024]{1,0:T(8,128)(2,1)S(1)}, bf16[256,1024]{1,0:T(8,128)(2,1)S(1)}, u32[]{:S(2)}, u32[]{:S(2)}) %collective-permute-start.13) | collective-permute-done | bytes 524320 | tf_op jit(solution)/shard_map/ppermute | solution.py:769
  164.9 10.2 %collective-permute-done.14.refs_2_ = bf16[256,1024]{1,0:T(8,128)(2,1)S(1)} collective-permute-done((bf16[256,1024]{1,0:T(8,128)(2,1)}, bf16[256,1024]{1,0:T(8,128)(2,1)S(1)}, u32[]{:S(2)}, u32[]{:S(2)}) %collective-permute-start.14) | collective-permute-done | bytes 524320 | tf_op jit(solution)/shard_map/ppermute | solution.py:769
  176.2 16.1 %mlp_back.3 = (bf16[1024,1024]{1,0:T(8,128)(2,1)}, bf16[1024,1024]{1,0:T(8,128)(2,1)}, bf16[1024,1024]{1,0:T(8,128)(2,1)}, f32[2,1024]{1,0:T(2,128)}, bf16[512,1...) custom-call(bf16[256,1024]{1,0:T(8,128)(2,1)} %copy-done.36, bf16[256,1024]{1,0:T(8,128)(2,1)} %copy-done.35, ...), custom_call_target="tpu_custom_call" | custom-call | tf_op jit(solution)/shard_map/mlp_back/pallas_call | solution.py:536
  193.7 16.4 %mlp_back.2 = (bf16[1024,1024]{1,0:T(8,128)(2,1)}, bf16[1024,1024]{1,0:T(8,128)(2,1)}, bf16[1024,1024]{1,0:T(8,128)(2,1)}, f32[2,1024]{1,0:T(2,128)}, bf16[512,1...) custom-call(bf16[256,1024]{1,0:T(8,128)(2,1)} %copy-done.34, bf16[256,1024]{1,0:T(8,128)(2,1)} %copy-done.33, ...), custom_call_target="tpu_custom_call" | custom-call | tf_op jit(solution)/shard_map/mlp_back/pallas_call | solution.py:536
  217.2 8.0 %collective-permute-done.23.refs_2_ = bf16[256,1024]{1,0:T(8,128)(2,1)S(1)} collective-permute-done((bf16[256,1024]{1,0:T(8,128)(2,1)S(1)}, bf16[256,1024]{1,0:T(8,128)(2,1)S(1)}, u32[]{:S(2)}, u32[]{:S(2)}) %collective-permute-start.23) | collective-permute-done | bytes 524320 | tf_op jit(solution)/shard_map/ppermute | solution.py:769
  248.3 10.2 %collective-permute-done.24.refs_2_ = bf16[256,1024]{1,0:T(8,128)(2,1)S(1)} collective-permute-done((bf16[256,1024]{1,0:T(8,128)(2,1)}, bf16[256,1024]{1,0:T(8,128)(2,1)S(1)}, u32[]{:S(2)}, u32[]{:S(2)}) %collective-permute-start.24) | collective-permute-done | bytes 524320 | tf_op jit(solution)/shard_map/ppermute | solution.py:769
  260.0 18.1 %attend_back.3 = (f32[1024,256]{1,0:T(8,128)}, f32[2048,256]{1,0:T(8,128)}, f32[2048,256]{1,0:T(8,128)}, f32[1024,256]{1,0:T(8,128)}) custom-call(s32[4]{0:T(128)} %get-tuple-element.181.tiles, s32[4]{0:T(128)} %get-tuple-element.164.starts, bf16[256,1024]{1,0:T(8,128)(2,1)} %collective-permute-done.28.refs_0_, bf16[256,1024]{1,0:T(8,128)(2,1)} %copy-done.28, ...), custom_call_target="tpu_custom_call" | custom-call | tf_op jit(solution)/shard_map/attend_back/pallas_call | solution.py:306
  279.1 13.9 %attend_back.2 = (f32[1024,256]{1,0:T(8,128)}, f32[2048,256]{1,0:T(8,128)}, f32[2048,256]{1,0:T(8,128)}, f32[1024,256]{1,0:T(8,128)}) custom-call(s32[4]{0:T(128)} %get-tuple-element.169.tiles, s32[4]{0:T(128)} %get-tuple-element.163.starts, bf16[256,1024]{1,0:T(8,128)(2,1)} %copy-done.27, bf16[256,1024]{1,0:T(8,128)(2,1)} %copy-done.26, ...), custom_call_target="tpu_custom_call" | custom-call | tf_op jit(solution)/shard_map/attend_back/pallas_call | solution.py:306
  294.4 19.9 %project_back.1 = (bf16[1024,1024]{1,0:T(8,128)(2,1)}, bf16[1024,1024]{1,0:T(8,128)(2,1)}, f32[1,256]{1,0:T(1,128)}, bf16[1024,768]{1,0:T(8,128)(2,1)}) custom-call(s32[8]{0:T(128)} %add.210.order, bf16[2048,1024]{1,0:T(8,128)(2,1)} %bitcast.79, f32[2048,256]{1,0:T(8,128)} %get-tuple-element.120.refs_1_, f32[2048,256]{1,0:T(8,128)} %get-tuple-element.121.refs_2_, ...), custom_call_target="tpu_custom_call" | custom-call | tf_op jit(solution)/shard_map/project_back/pallas_call | solution.py:670
  318.7 9.2 %outer.3 = bf16[1024,1024]{1,0:T(8,128)(2,1)} custom-call(bf16[1024,1024]{1,0:T(8,128)(2,1)} %get-tuple-element.139.refs_0_, bf16[1024,1024]{1,0:T(8,128)(2,1)} %get-tuple-element.140.refs_1_, bf16[1024,1024]{1,0:T(8,128)(2,1)} %get-tuple-element.141.refs_2_, bf16[1024,1024]{1,0:T(8,128)(2,1)} %get-tuple-element.142.refs_3_), custom_call_target="tpu_custom_call" | custom-call | tf_op jit(solution)/shard_map/outer/pallas_call | solution.py:717
  327.9 8.9 %outer.4 = bf16[1024,1024]{1,0:T(8,128)(2,1)} custom-call(bf16[1024,1024]{1,0:T(8,128)(2,1)} %get-tuple-element.139.refs_0_, bf16[1024,1024]{1,0:T(8,128)(2,1)} %get-tuple-element.140.refs_1_, bf16[1024,1024]{1,0:T(8,128)(2,1)} %get-tuple-element.143.refs_2_, bf16[1024,1024]{1,0:T(8,128)(2,1)} %get-tuple-element.144.refs_3_), custom_call_target="tpu_custom_call" | custom-call | tf_op jit(solution)/shard_map/outer/pallas_call | solution.py:717
  336.7 9.0 %outer.5 = bf16[1024,1024]{1,0:T(8,128)(2,1)} custom-call(bf16[1024,1024]{1,0:T(8,128)(2,1)} %get-tuple-element.145.refs_0_, bf16[1024,1024]{1,0:T(8,128)(2,1)} %get-tuple-element.146.refs_1_, bf16[1024,1024]{1,0:T(8,128)(2,1)} %get-tuple-element.147.refs_2_, bf16[1024,1024]{1,0:T(8,128)(2,1)} %get-tuple-element.148.refs_3_), custom_call_target="tpu_custom_call" | custom-call | tf_op jit(solution)/shard_map/outer/pallas_call | solution.py:717
  363.0 56.9 %reduce-scatter.3.cloned.1.call-done = bf16[1,1024,128]{2,1,0:T(8,128)(2,1)} async-done(((bf16[8,1024,128]{2,1,0:T(8,128)(2,1)}), bf16[1,1024,128]{2,1,0:T(8,128)(2,1)}) %reduce-scatter.3.cloned.1.call-update) | async-done | bytes 262160 | tf_op jit(solution)/shard_map/reduce_scatter | solution.py:965
  419.9 120.6 %reduce-scatter.5.cloned.1.call-done = bf16[1,3072,128]{2,1,0:T(8,128)(2,1)} async-done(((bf16[8,3072,128]{2,1,0:T(8,128)(2,1)}), bf16[1,3072,128]{2,1,0:T(8,128)(2,1)}) %reduce-scatter.5.cloned.1.call-update) | async-done | bytes 786448 | tf_op jit(solution)/shard_map/reduce_scatter | solution.py:965
  558.7 7.2 %collective-permute-done.41 = f32[4096]{0:T(1024)S(1)} collective-permute-done((f32[4096]{0:T(1024)S(1)}, f32[4096]{0:T(1024)S(1)}, u32[]{:S(2)}, u32[]{:S(2)}) %collective-permute-start.41) | collective-permute-done | bytes 16416 | tf_op jit(solution)/shard_map/ppermute | solution.py:769
  587.1 7.2 %step.1 = (f32[32,128,128]{2,1,0:T(8,128)}, f32[32,128,128]{2,1,0:T(8,128)}, f32[32,128]{1,0:T(8,128)}) custom-call(bf16[8,32,16,128]{3,2,1,0:T(8,128)(2,1)} %copy-done, f32[32,128,128]{2,1,0:T(8,128)} %bitcast.87, f32[32,128,128]{2,1,0:T(8,128)} %bitcast.88, f32[32,128,128]{2,1,0:T(8,128)} %bitcast.89), custom_call_target="tpu_custom_call" | custom-call | tf_op jit(solution)/shard_map/step/pallas_call | solution.py:993
  609.6 5.6 stats.1
  (257 shorter events, 187.4 us)
Async XLA Ops:
  7.2 412.7 %reduce-scatter.3.cloned.1.call-start = ((), (), s32[]{:S(2)}) async-start(), calls=%async_computation.3 | async-start | bytes 2359296 | tf_op jit(solution)/shard_map/reduce_scatter | solution.py:965
  47.7 15.9 %collective-permute-start.8 = (bf16[256,1024]{1,0:T(8,128)(2,1)}, bf16[256,1024]{1,0:T(8,128)(2,1)}, u32[]{:S(2)}, u32[]{:S(2)}) collective-permute-start(bf16[256,1024]{1,0:T(8,128)(2,1)} %add_convert_fusion.5), channel_id=1, source_target_pairs={{0,16},{8,24},{16,0},{24,8},{1,17},{9,25},{17,1},{25,9},{2,18},{10... | collective-permute-start | bytes 1572872 | tf_op jit(solution)/shard_map/ppermute | solution.py:769
  52.1 22.6 %collective-permute-start.1 = (bf16[256,1024]{1,0:T(8,128)(2,1)S(1)}, bf16[256,1024]{1,0:T(8,128)(2,1)S(1)}, u32[]{:S(2)}, u32[]{:S(2)}) collective-permute-start(bf16[256,1024]{1,0:T(8,128)(2,1)S(1)} %add_convert_fusion.7), channel_id=1, source_target_pairs={{0,16},{8,24},{16,0},{24,8},{1,17},{9,25},{17,1},{25,9},{2,18},{10... | collective-permute-start | bytes 1572872 | tf_op jit(solution)/shard_map/ppermute | solution.py:769
  68.0 18.0 %collective-permute-start.9 = (bf16[256,1024]{1,0:T(8,128)(2,1)}, bf16[256,1024]{1,0:T(8,128)(2,1)S(1)}, u32[]{:S(2)}, u32[]{:S(2)}) collective-permute-start(bf16[256,1024]{1,0:T(8,128)(2,1)} %get-tuple-element.99.refs_3_), channel_id=1, source_target_pairs={{0,16},{8,24},{16,0},{24,8},{1,17},{9,25},{17,1},{25,9},{2,18},{10... | collective-permute-start | bytes 1572872 | tf_op jit(solution)/shard_map/ppermute | solution.py:769
  80.0 16.7 %collective-permute-start.2 = (bf16[256,1024]{1,0:T(8,128)(2,1)}, bf16[256,1024]{1,0:T(8,128)(2,1)S(1)}, u32[]{:S(2)}, u32[]{:S(2)}) collective-permute-start(bf16[256,1024]{1,0:T(8,128)(2,1)} %get-tuple-element.92.refs_3_), channel_id=1, source_target_pairs={{0,16},{8,24},{16,0},{24,8},{1,17},{9,25},{17,1},{25,9},{2,18},{10... | collective-permute-start | bytes 1572872 | tf_op jit(solution)/shard_map/ppermute | solution.py:769
  86.0 26.2 %collective-permute-start.4 = (bf16[256,1024]{1,0:T(8,128)(2,1)}, bf16[256,1024]{1,0:T(8,128)(2,1)S(1)}, u32[]{:S(2)}, u32[]{:S(2)}) collective-permute-start(bf16[256,1024]{1,0:T(8,128)(2,1)} %get-tuple-element.92.refs_3_), channel_id=1, source_target_pairs={{0,8},{8,0},{16,24},{24,16},{1,9},{9,1},{17,25},{25,17},{2,10},{10... | collective-permute-start | bytes 1572872 | tf_op jit(solution)/shard_map/ppermute | solution.py:769
  96.7 15.5 %collective-permute-start.3 = (bf16[256,1024]{1,0:T(8,128)(2,1)S(1)}, bf16[256,1024]{1,0:T(8,128)(2,1)}, u32[]{:S(2)}, u32[]{:S(2)}) collective-permute-start(bf16[256,1024]{1,0:T(8,128)(2,1)S(1)} %collective-permute-done.2.refs_2_), channel_id=1, source_target_pairs={{0,8},{8,0},{16,24},{24,16},{1,9},{9,1},{17,25},{25,17},{2,10},{10... | collective-permute-start | bytes 1572872 | tf_op jit(solution)/shard_map/ppermute | solution.py:769
  111.6 15.2 %collective-permute-start.12 = (bf16[512,1024]{1,0:T(8,128)(2,1)}, bf16[512,1024]{1,0:T(8,128)(2,1)S(1)}, u32[]{:S(2)}, u32[]{:S(2)}) collective-permute-start(bf16[512,1024]{1,0:T(8,128)(2,1)} %get-tuple-element.101), channel_id=1, source_target_pairs={{0,8},{8,0},{16,24},{24,16},{1,9},{9,1},{17,25},{25,17},{2,10},{10... | collective-permute-start | bytes 3145736 | tf_op jit(solution)/shard_map/ppermute | solution.py:769
  132.1 21.0 %collective-permute-start.6 = (bf16[256,1024]{1,0:T(8,128)(2,1)}, bf16[256,1024]{1,0:T(8,128)(2,1)S(1)}, u32[]{:S(2)}, u32[]{:S(2)}) collective-permute-start(bf16[256,1024]{1,0:T(8,128)(2,1)} %add_convert_fusion.6), channel_id=1, source_target_pairs={{0,16},{8,24},{16,0},{24,8},{1,17},{9,25},{17,1},{25,9},{2,18},{10... | collective-permute-start | bytes 1572872 | tf_op jit(solution)/shard_map/ppermute | solution.py:769
  147.7 16.7 %collective-permute-start.19 = (bf16[256,1024]{1,0:T(8,128)(2,1)}, bf16[256,1024]{1,0:T(8,128)(2,1)S(1)}, u32[]{:S(2)}, u32[]{:S(2)}) collective-permute-start(bf16[256,1024]{1,0:T(8,128)(2,1)} %get-tuple-element.112.refs_3_), channel_id=1, source_target_pairs={{0,16},{8,24},{16,0},{24,8},{1,17},{9,25},{17,1},{25,9},{2,18},{10... | collective-permute-start | bytes 1572872 | tf_op jit(solution)/shard_map/ppermute | solution.py:769
  159.0 16.1 %collective-permute-start.14 = (bf16[256,1024]{1,0:T(8,128)(2,1)}, bf16[256,1024]{1,0:T(8,128)(2,1)S(1)}, u32[]{:S(2)}, u32[]{:S(2)}) collective-permute-start(bf16[256,1024]{1,0:T(8,128)(2,1)} %get-tuple-element.104.refs_3_), channel_id=1, source_target_pairs={{0,16},{8,24},{16,0},{24,8},{1,17},{9,25},{17,1},{25,9},{2,18},{10... | collective-permute-start | bytes 1572872 | tf_op jit(solution)/shard_map/ppermute | solution.py:769
  164.4 28.4 %collective-permute-start.16 = (bf16[256,1024]{1,0:T(8,128)(2,1)}, bf16[256,1024]{1,0:T(8,128)(2,1)S(1)}, u32[]{:S(2)}, u32[]{:S(2)}) collective-permute-start(bf16[256,1024]{1,0:T(8,128)(2,1)} %get-tuple-element.104.refs_3_), channel_id=1, source_target_pairs={{0,8},{8,0},{16,24},{24,16},{1,9},{9,1},{17,25},{25,17},{2,10},{10... | collective-permute-start | bytes 1572872 | tf_op jit(solution)/shard_map/ppermute | solution.py:769
  175.1 17.7 %collective-permute-start.15 = (bf16[256,1024]{1,0:T(8,128)(2,1)S(1)}, bf16[256,1024]{1,0:T(8,128)(2,1)S(1)}, u32[]{:S(2)}, u32[]{:S(2)}) collective-permute-start(bf16[256,1024]{1,0:T(8,128)(2,1)S(1)} %collective-permute-done.14.refs_2_), channel_id=1, source_target_pairs={{0,8},{8,0},{16,24},{24,16},{1,9},{9,1},{17,25},{25,17},{2,10},{10... | collective-permute-start | bytes 1572872 | tf_op jit(solution)/shard_map/ppermute | solution.py:769
  192.2 18.0 %collective-permute-start.22 = (bf16[512,1024]{1,0:T(8,128)(2,1)}, bf16[512,1024]{1,0:T(8,128)(2,1)S(1)}, u32[]{:S(2)}, u32[]{:S(2)}) collective-permute-start(bf16[512,1024]{1,0:T(8,128)(2,1)} %get-tuple-element.116), channel_id=1, source_target_pairs={{0,8},{8,0},{16,24},{24,16},{1,9},{9,1},{17,25},{25,17},{2,10},{10... | collective-permute-start | bytes 3145736 | tf_op jit(solution)/shard_map/ppermute | solution.py:769
  215.5 21.0 %collective-permute-start.18 = (bf16[256,1024]{1,0:T(8,128)(2,1)}, bf16[256,1024]{1,0:T(8,128)(2,1)S(1)}, u32[]{:S(2)}, u32[]{:S(2)}) collective-permute-start(bf16[256,1024]{1,0:T(8,128)(2,1)} %add_convert_fusion.3), channel_id=1, source_target_pairs={{0,16},{8,24},{16,0},{24,8},{1,17},{9,25},{17,1},{25,9},{2,18},{10... | collective-permute-start | bytes 1572872 | tf_op jit(solution)/shard_map/ppermute | solution.py:769
  231.2 16.6 %collective-permute-start.27 = (bf16[256,1024]{1,0:T(8,128)(2,1)}, bf16[256,1024]{1,0:T(8,128)(2,1)S(1)}, u32[]{:S(2)}, u32[]{:S(2)}) collective-permute-start(bf16[256,1024]{1,0:T(8,128)(2,1)} %get-tuple-element.126.refs_3_), channel_id=1, source_target_pairs={{0,16},{8,24},{16,0},{24,8},{1,17},{9,25},{17,1},{25,9},{2,18},{10... | collective-permute-start | bytes 1572872 | tf_op jit(solution)/shard_map/ppermute | solution.py:769
  242.4 16.1 %collective-permute-start.24 = (bf16[256,1024]{1,0:T(8,128)(2,1)}, bf16[256,1024]{1,0:T(8,128)(2,1)S(1)}, u32[]{:S(2)}, u32[]{:S(2)}) collective-permute-start(bf16[256,1024]{1,0:T(8,128)(2,1)} %get-tuple-element.122.refs_3_), channel_id=1, source_target_pairs={{0,16},{8,24},{16,0},{24,8},{1,17},{9,25},{17,1},{25,9},{2,18},{10... | collective-permute-start | bytes 1572872 | tf_op jit(solution)/shard_map/ppermute | solution.py:769
  247.7 30.4 %collective-permute-start.26 = (bf16[256,1024]{1,0:T(8,128)(2,1)}, bf16[256,1024]{1,0:T(8,128)(2,1)S(1)}, u32[]{:S(2)}, u32[]{:S(2)}) collective-permute-start(bf16[256,1024]{1,0:T(8,128)(2,1)} %get-tuple-element.122.refs_3_), channel_id=1, source_target_pairs={{0,8},{8,0},{16,24},{24,16},{1,9},{9,1},{17,25},{25,17},{2,10},{10... | collective-permute-start | bytes 1572872 | tf_op jit(solution)/shard_map/ppermute | solution.py:769
  258.5 19.7 %collective-permute-start.25 = (bf16[256,1024]{1,0:T(8,128)(2,1)S(1)}, bf16[256,1024]{1,0:T(8,128)(2,1)S(1)}, u32[]{:S(2)}, u32[]{:S(2)}) collective-permute-start(bf16[256,1024]{1,0:T(8,128)(2,1)S(1)} %collective-permute-done.24.refs_2_), channel_id=1, source_target_pairs={{0,8},{8,0},{16,24},{24,16},{1,9},{9,1},{17,25},{25,17},{2,10},{10... | collective-permute-start | bytes 1572872 | tf_op jit(solution)/shard_map/ppermute | solution.py:769
  318.6 221.9 %reduce-scatter.5.cloned.1.call-start = ((), (), s32[]{:S(2)}) async-start(), calls=%async_computation.4 | async-start | bytes 7077888 | tf_op jit(solution)/shard_map/reduce_scatter | solution.py:965
  356.5 217.9 %collective-permute-start.30 = (bf16[1024,1024]{1,0:T(8,128)(2,1)}, bf16[1024,1024]{1,0:T(8,128)(2,1)}, u32[]{:S(2)}, u32[]{:S(2)}) collective-permute-start(bf16[1024,1024]{1,0:T(8,128)(2,1)} %get-tuple-element.135), channel_id=1, source_target_pairs={{0,8},{8,0},{16,24},{24,16},{1,9},{9,1},{17,25},{25,17},{2,10},{10... | collective-permute-start | bytes 6291464 | tf_op jit(solution)/shard_map/ppermute | solution.py:769
  361.2 186.6 %collective-permute-start.39 = (f32[2,1024]{1,0:T(2,128)S(1)}, f32[2,1024]{1,0:T(2,128)S(1)}, u32[]{:S(2)}, u32[]{:S(2)}) collective-permute-start(f32[2,1024]{1,0:T(2,128)S(1)} %fusion.14), channel_id=1, source_target_pairs={{0,16},{8,24},{16,0},{24,8},{1,17},{9,25},{17,1},{25,9},{2,18},{10... | collective-permute-start | bytes 24584 | tf_op jit(solution)/shard_map/ppermute | solution.py:769
  543.9 42.2 %all-to-all-start = ((bf16[8,32,16,128]{3,2,1,0:T(8,128)(2,1)}), bf16[8,32,16,128]{3,2,1,0:T(8,128)(2,1)S(1)}, u32[]{:S(2)}, u32[]{:S(2)}) async-start(bf16[8,32,16,128]{3,2,1,0:T(8,128)(2,1)} %broadcast_select_fusion), calls=%async_computation.2 | async-start | bytes 2097152 | tf_op jit(solution)/shard_map/all_to_all | solution.py:976
  577.0 28.4 %collective-permute-start.31 = (bf16[512,1024]{1,0:T(8,128)(2,1)}, bf16[512,1024]{1,0:T(8,128)(2,1)}, u32[]{:S(2)}, u32[]{:S(2)}) collective-permute-start(bf16[512,1024]{1,0:T(8,128)(2,1)} %add_convert_fusion), channel_id=1, source_target_pairs={{0,16},{8,24},{16,0},{24,8},{1,17},{9,25},{17,1},{25,9},{2,18},{10... | collective-permute-start | bytes 3145736 | tf_op jit(solution)/shard_map/ppermute | solution.py:769
  (70 other events, 536.9 us)
Sparse Core Ops, SparseCore 0:
  318.8 101.0 reduce-scatter.2
  423.5 116.9 reduce-scatter.4
